TPU v7x, 768 devices: a whole 4x8x12 slice. The times are simulated.
768 devices in a mesh: outer: 16 (over y_lo, x, core), inner: 48 (over z, y_hi).
Axes of the slice: x: 4, y: 8 (y_hi: 4, y_lo: 2; y = y_hi * 2 + y_lo), z: 12, core: 2. Of those that a mesh axis runs over, the one named last changes fastest.
Arguments:
- vertex: float32 [196608, 1024], P(('outer', 'inner')), may hold values from -1.5 to 1.5
- vertex_state: float32 [196608], P(('outer', 'inner')), may hold values from 0.05 to 0.5
- context: float32 [196608, 1024], P(('outer', 'inner')), may hold values from -1.5 to 1.5
- context_state: float32 [196608], P(('outer', 'inner')), may hold values from 0.05 to 0.5
- edge_source: int32 [768, 1536], P(('outer', 'inner')), may hold values from 0 to 255
- edge_target: int32 [768, 1536], P(('outer', 'inner')), may hold values from 0 to 255
Outputs:
- vertex_out: float32 [196608, 1024], P(('outer', 'inner'))
- vertex_state_out: float32 [196608], P(('outer', 'inner'))
- context_out: float32 [196608, 1024], P(('outer', 'inner'))
- context_state_out: float32 [196608], P(('outer', 'inner'))
All inputs are finite; a program needn't handle non-finite values.
Results may differ from a plain program's by a relative error of at most 0.0019.
Values sent between devices are 32-bit elements; how exact they have to be, the bound alone decides.
No kernel may reach another device: no remote copies, remote signals or barrier semaphores. Data moves between devices by JAX's collectives and lax.ppermute only.
A program may use at most 32 MiB of HBM per device.

v0:
```python
import jax
import jax.numpy as jnp
from jax import lax
from jax.sharding import PartitionSpec as P

ROUNDS = 3


def from_behind(array, axis, by):
    size = lax.axis_size(axis)
    return lax.ppermute(array, axis, [(i, (i + by) % size) for i in range(size)])


def edge_counts(source, target, row_count, block_rows):
    source_hot = (source[:, None] == jnp.arange(row_count, dtype=jnp.int32)[None, :]).astype(
        jnp.bfloat16
    )
    target_hot = (target[:, None] == jnp.arange(block_rows, dtype=jnp.int32)[None, :]).astype(
        jnp.bfloat16
    )
    return jnp.dot(source_hot.T, target_hot, preferred_element_type=jnp.float32)


def gradient(rows_b, block_b, source, target):
    scores = jnp.dot(rows_b, block_b.T, preferred_element_type=jnp.float32)
    prob = jax.nn.sigmoid(scores)
    counts = edge_counts(source, target, rows_b.shape[0], block_b.shape[0])
    return (prob / block_b.shape[0] - counts * (1.0 - prob)).astype(jnp.bfloat16)


def adagrad(weights, state, grad):
    state = state + jnp.mean(grad * grad, axis=1)
    return (weights - 0.1 * grad / jnp.sqrt(state)[:, None], state)


def body(vertex, vertex_state, context, context_state, edge_source, edge_target):
    rows, row_state = (vertex, vertex_state)
    block, block_state = (context, context_state)
    edges = edge_source.shape[1] // ROUNDS
    for step in range(ROUNDS):
        source = edge_source[0, step * edges : (step + 1) * edges]
        target = edge_target[0, step * edges : (step + 1) * edges]
        if step > 0:
            block, block_state = from_behind((block, block_state), "inner", 1)
        rows_b = rows.astype(jnp.bfloat16)
        block_b = block.astype(jnp.bfloat16)
        grad = gradient(rows_b, block_b, source, target)
        block_grad = jnp.dot(grad.T, rows_b, preferred_element_type=jnp.float32)
        rows_grad = jnp.dot(grad, block_b, preferred_element_type=jnp.float32)
        block, block_state = adagrad(block, block_state, block_grad)
        rows, row_state = adagrad(rows, row_state, rows_grad)
        if step == ROUNDS - 1:
            block, block_state = from_behind((block, block_state), "outer", 1)
    return (rows, row_state, block, block_state)


def solution(mesh):
    placed = (
        P(("outer", "inner"), None),
        P(("outer", "inner")),
        P(("outer", "inner"), None),
        P(("outer", "inner")),
        P(("outer", "inner"), None),
        P(("outer", "inner"), None),
    )
    return jax.shard_map(
        body,
        mesh=mesh,
        in_specs=placed,
        out_specs=(
            P(("outer", "inner"), None),
            P(("outer", "inner")),
            P(("outer", "inner"), None),
            P(("outer", "inner")),
        ),
        check_vma=False,
    )
```

profile of v0, /device:TPU:56, one launch (start us, length us, event | category | flops | bytes accessed | tf_op | source)
XLA Modules:
  0.0 150.1 jit_solution(16893094262128390479)
XLA Ops:
  0.6 0.0 copy-start.3
  0.6 0.7 fusion.45
  1.4 0.0 copy-done.3
  1.4 0.0 copy-start.1
  1.4 2.0 %fusion.7 = f32[256,256]{1,0:T(8,128)S(1)} fusion(f32[256,1024]{1,0:T(8,128)} %param.8, f32[256,1024]{1,0:T(8,128)} %param.6), kind=kOutput, calls=%fused_computation.13 | convolution fusion | flops 134938624 | bytes 2359296 | tf_op jit(solution)/shard_map/dot_general | solution.py:25
  3.4 0.5 fusion.12
  3.9 0.0 copy-done.1
  3.9 0.0 copy-start
  3.9 0.4 multiply_reduce_fusion.4
  4.3 0.0 copy-start.4
  4.3 0.7 copy-done.4
  5.0 0.1 copy-done
  5.1 0.3 divide_subtract_fusion.4
  5.4 4.5 %collective-permute-start = (f32[256,1024]{1,0:T(8,128)S(1)}, f32[256,1024]{1,0:T(8,128)S(1)}, u32[]{:S(2)}, u32[]{:S(2)}) collective-permute-start(f32[256,1024]{1,0:T(8,128)S(1)} %divide_subtract_fusion.4), channel_id=1, source_target_pairs={{0,1},{1,2},{2,3},{3,4},{4,5},{5,6},{6,7},{7,8},{8,9},{9,10},{10,1... | collective-permute-start | bytes 3145736 | tf_op jit(solution)/shard_map/ppermute | solution.py:11
  9.9 4.5 %collective-permute-start.1 = (f32[256]{0:T(256)S(1)}, f32[256]{0:T(256)S(1)}, u32[]{:S(2)}, u32[]{:S(2)}) collective-permute-start(f32[256]{0:T(256)S(1)} %get-tuple-element.11), channel_id=1, source_target_pairs={{0,1},{1,2},{2,3},{3,4},{4,5},{5,6},{6,7},{7,8},{8,9},{9,10},{10,1... | collective-permute-start | bytes 3080 | tf_op jit(solution)/shard_map/ppermute | solution.py:11
  14.4 0.4 multiply_reduce_fusion.5
  14.8 0.0 copy-start.2
  14.8 0.7 copy-done.2
  15.5 0.3 divide_subtract_fusion.5
  15.7 72.5 %collective-permute-done = f32[256,1024]{1,0:T(8,128)S(1)} collective-permute-done((f32[256,1024]{1,0:T(8,128)S(1)}, f32[256,1024]{1,0:T(8,128)S(1)}, u32[]{:S(2)}, u32[]{:S(2)}) %collective-permute-start) | collective-permute-done | bytes 1048608 | tf_op jit(solution)/shard_map/ppermute | solution.py:11
  88.3 0.4 fusion.9
  88.6 0.5 fusion.13
  89.1 0.4 multiply_reduce_fusion.2
  89.5 0.0 collective-permute-done.1
  89.5 0.3 divide_subtract_fusion.2
  89.8 1.9 %collective-permute-start.2 = (f32[256,1024]{1,0:T(8,128)S(1)}, f32[256,1024]{1,0:T(8,128)S(1)}, u32[]{:S(2)}, u32[]{:S(2)}) collective-permute-start(f32[256,1024]{1,0:T(8,128)S(1)} %divide_subtract_fusion.2), channel_id=1, source_target_pairs={{0,1},{1,2},{2,3},{3,4},{4,5},{5,6},{6,7},{7,8},{8,9},{9,10},{10,1... | collective-permute-start | bytes 3145736 | tf_op jit(solution)/shard_map/ppermute | solution.py:11
  91.8 1.9 %collective-permute-start.3 = (f32[256]{0:T(256)S(1)}, f32[256]{0:T(256)S(1)}, u32[]{:S(2)}, u32[]{:S(2)}) collective-permute-start(f32[256]{0:T(256)S(1)} %get-tuple-element.9), channel_id=1, source_target_pairs={{0,1},{1,2},{2,3},{3,4},{4,5},{5,6},{6,7},{7,8},{8,9},{9,10},{10,1... | collective-permute-start | bytes 3080 | tf_op jit(solution)/shard_map/ppermute | solution.py:11
  93.7 0.4 multiply_reduce_fusion.3
  94.1 0.3 divide_subtract_fusion.3
  94.4 34.3 %collective-permute-done.2 = f32[256,1024]{1,0:T(8,128)S(1)} collective-permute-done((f32[256,1024]{1,0:T(8,128)S(1)}, f32[256,1024]{1,0:T(8,128)S(1)}, u32[]{:S(2)}, u32[]{:S(2)}) %collective-permute-start.2) | collective-permute-done | bytes 1048608 | tf_op jit(solution)/shard_map/ppermute | solution.py:11
  128.7 0.4 fusion.11
  129.1 0.5 fusion.14
  129.6 0.4 multiply_reduce_fusion
  130.0 0.0 collective-permute-done.3
  130.0 0.3 divide_subtract_fusion
  130.3 1.9 %collective-permute-start.4 = (f32[256,1024]{1,0:T(8,128)S(1)}, f32[256,1024]{1,0:T(8,128)S(1)}, u32[]{:S(2)}, u32[]{:S(2)}) collective-permute-start(f32[256,1024]{1,0:T(8,128)S(1)} %divide_subtract_fusion), channel_id=1, source_target_pairs={{0,48},{48,96},{96,144},{144,192},{192,240},{240,288},{288,336},{3... | collective-permute-start | bytes 3145736 | tf_op jit(solution)/shard_map/ppermute | solution.py:11
  132.2 3.5 %collective-permute-start.5 = (f32[256]{0:T(256)S(1)}, f32[256]{0:T(256)S(1)}, u32[]{:S(2)}, u32[]{:S(2)}) collective-permute-start(f32[256]{0:T(256)S(1)} %get-tuple-element.5), channel_id=1, source_target_pairs={{0,48},{48,96},{96,144},{144,192},{192,240},{240,288},{288,336},{3... | collective-permute-start | bytes 3080 | tf_op jit(solution)/shard_map/ppermute | solution.py:11
  135.7 0.4 multiply_reduce_fusion.1
  136.1 0.6 fusion.42
  136.7 1.2 divide_subtract_fusion.1
  137.9 10.7 %collective-permute-done.5 = f32[256]{0:T(256)S(1)} collective-permute-done((f32[256]{0:T(256)S(1)}, f32[256]{0:T(256)S(1)}, u32[]{:S(2)}, u32[]{:S(2)}) %collective-permute-start.5) | collective-permute-done | bytes 1056 | tf_op jit(solution)/shard_map/ppermute | solution.py:11
  148.6 0.0 collective-permute-done.4
  148.6 1.0 copy.12
  149.5 0.6 copy.13
  (6 shorter events, 0.0 us)
Async XLA Ops:
  0.6 0.7 copy-start.3
  1.4 2.5 %copy-start.1 = (f32[256,1024]{1,0:T(8,128)S(1)}, f32[256,1024]{1,0:T(8,128)}, u32[]{:S(2)}) copy-start(f32[256,1024]{1,0:T(8,128)} %param.6) | copy-start | bytes 3145732
  3.9 1.2 copy-start
  4.3 0.7 copy-start.4
  5.4 82.9 %collective-permute-start = (f32[256,1024]{1,0:T(8,128)S(1)}, f32[256,1024]{1,0:T(8,128)S(1)}, u32[]{:S(2)}, u32[]{:S(2)}) collective-permute-start(f32[256,1024]{1,0:T(8,128)S(1)} %divide_subtract_fusion.4), channel_id=1, source_target_pairs={{0,1},{1,2},{2,3},{3,4},{4,5},{5,6},{6,7},{7,8},{8,9},{9,10},{10,1... | collective-permute-start | bytes 3145736 | tf_op jit(solution)/shard_map/ppermute | solution.py:11
  9.9 79.7 %collective-permute-start.1 = (f32[256]{0:T(256)S(1)}, f32[256]{0:T(256)S(1)}, u32[]{:S(2)}, u32[]{:S(2)}) collective-permute-start(f32[256]{0:T(256)S(1)} %get-tuple-element.11), channel_id=1, source_target_pairs={{0,1},{1,2},{2,3},{3,4},{4,5},{5,6},{6,7},{7,8},{8,9},{9,10},{10,1... | collective-permute-start | bytes 3080 | tf_op jit(solution)/shard_map/ppermute | solution.py:11
  14.8 0.7 copy-start.2
  89.8 38.9 %collective-permute-start.2 = (f32[256,1024]{1,0:T(8,128)S(1)}, f32[256,1024]{1,0:T(8,128)S(1)}, u32[]{:S(2)}, u32[]{:S(2)}) collective-permute-start(f32[256,1024]{1,0:T(8,128)S(1)} %divide_subtract_fusion.2), channel_id=1, source_target_pairs={{0,1},{1,2},{2,3},{3,4},{4,5},{5,6},{6,7},{7,8},{8,9},{9,10},{10,1... | collective-permute-start | bytes 3145736 | tf_op jit(solution)/shard_map/ppermute | solution.py:11
  91.8 38.2 %collective-permute-start.3 = (f32[256]{0:T(256)S(1)}, f32[256]{0:T(256)S(1)}, u32[]{:S(2)}, u32[]{:S(2)}) collective-permute-start(f32[256]{0:T(256)S(1)} %get-tuple-element.9), channel_id=1, source_target_pairs={{0,1},{1,2},{2,3},{3,4},{4,5},{5,6},{6,7},{7,8},{8,9},{9,10},{10,1... | collective-permute-start | bytes 3080 | tf_op jit(solution)/shard_map/ppermute | solution.py:11
  130.3 18.3 %collective-permute-start.4 = (f32[256,1024]{1,0:T(8,128)S(1)}, f32[256,1024]{1,0:T(8,128)S(1)}, u32[]{:S(2)}, u32[]{:S(2)}) collective-permute-start(f32[256,1024]{1,0:T(8,128)S(1)} %divide_subtract_fusion), channel_id=1, source_target_pairs={{0,48},{48,96},{96,144},{144,192},{192,240},{240,288},{288,336},{3... | collective-permute-start | bytes 3145736 | tf_op jit(solution)/shard_map/ppermute | solution.py:11
  132.2 16.3 %collective-permute-start.5 = (f32[256]{0:T(256)S(1)}, f32[256]{0:T(256)S(1)}, u32[]{:S(2)}, u32[]{:S(2)}) collective-permute-start(f32[256]{0:T(256)S(1)} %get-tuple-element.5), channel_id=1, source_target_pairs={{0,48},{48,96},{96,144},{144,192},{192,240},{240,288},{288,336},{3... | collective-permute-start | bytes 3080 | tf_op jit(solution)/shard_map/ppermute | solution.py:11
where the time goes:
time: 150 us
  waiting for transfers between devices  118 us (79%)
  starting transfers between devices  18.2 us (12%)
  matrix products  6.51 us (4%)
  local copies, waits for them, and re-layouts  3.74 us (2%)
  other arithmetic  3.21 us (2%)
    ppermute x6, waiting for transfers between devices, from_behind(): lax.ppermute(array, axis, [(i, (i + by) % size) for i in range(size)])  118 us
    ppermute x6, starting transfers between devices, from_behind(): lax.ppermute(array, axis, [(i, (i + by) % size) for i in range(size)])  18.2 us
    unnamed x12, local copies, waits for them, and re-layouts  3.02 us
  transfers between devices with their start and end apart: 6, of which 3 were waited for; matrix products, arithmetic and copies ran while one was open for 4% of the time, Pallas kernels for 0%

commit v1 on v0

v1 whole, which is shorter than its diff:
```python
import functools

import jax
import jax.numpy as jnp
from jax import lax
from jax.experimental import pallas as pl
from jax.experimental.pallas import tpu as pltpu
from jax.sharding import PartitionSpec as P

ROUNDS = 3
BOTH = ("outer", "inner")
CHUNKS = ((0, 144), (144, 112))
PAD = 8
VMEM = pl.BlockSpec(memory_space=pltpu.VMEM)


def places():
    return lax.axis_size("outer"), lax.axis_size("inner")


def step_inner(n_outer, n_inner):
    return [(o * n_inner + i, o * n_inner + (i + 1) % n_inner) for o in range(n_outer) for i in range(n_inner)]


def step_outer(n_outer, n_inner):
    return [(o * n_inner + i, (o + 1) % n_outer * n_inner + i) for o in range(n_outer) for i in range(n_inner)]


def dot(a, b, contract):
    return lax.dot_general(a, b, (contract, ((), ())), preferred_element_type=jnp.float32)


def hot(index, first, size):
    number = lax.broadcasted_iota(jnp.int32, (size, index.shape[1]), 0) + first
    return jnp.where(number == index, 1.0, 0.0).astype(jnp.bfloat16)


def own_rows(first, size, total):
    row = lax.broadcasted_iota(jnp.int32, (size, total), 0) + first
    return row == lax.broadcasted_iota(jnp.int32, (size, total), 1)


def meet_kernel(first, step, edges, fresh, carry, *refs):
    rows_ref, block_ref, state_ref, source_ref, target_ref, *refs = refs
    before_ref = None
    if first > 0:
        before_ref, *refs = refs
    new_ref, grad_ref, states_ref, *refs = refs
    rows_b = rows_ref[...].astype(jnp.bfloat16)
    if fresh:
        refs[0][...] = rows_b
    size, total = block_ref.shape[0], state_ref.shape[1]
    block = block_ref[...]
    prob = jax.nn.sigmoid(dot(block.astype(jnp.bfloat16), rows_b, ((1,), (1,))))
    window = pl.ds(step * edges, edges)
    counts = dot(hot(target_ref[:, window], first, size), hot(source_ref[:, window], 0, rows_b.shape[0]), ((1,), (1,)))
    grad = (prob / total - counts * (1.0 - prob)).astype(jnp.bfloat16)
    grad_ref[...] = grad
    block_grad = dot(grad, rows_b, ((1,), (0,)))
    mine = own_rows(first, size, total)
    state = jnp.sum(jnp.where(mine, state_ref[...], 0.0), axis=1, keepdims=True)
    state = state + jnp.mean(block_grad * block_grad, axis=1, keepdims=True)
    new_ref[pl.ds(0, size), :] = block - block_grad * (0.1 / jnp.sqrt(state))
    states = jnp.sum(jnp.where(mine, state, 0.0), axis=0, keepdims=True)
    if first > 0:
        states = states + before_ref[...]
    states_ref[...] = states
    if carry:
        new_ref[pl.ds(size, PAD), :] = jnp.zeros((PAD, new_ref.shape[1]), jnp.float32)
        new_ref[pl.ds(size, 1), pl.ds(0, total)] = states


def meet(rows, block, offset, state, source, target, before, first, size, step, last):
    fresh = offset is not None and first == 0
    carry = last and before is not None
    count, width = rows.shape
    edges = source.shape[1] // ROUNDS
    if offset is None:
        spec = VMEM
    else:
        spec = pl.BlockSpec((pl.Element(size), pl.Element(width)), lambda g: (offset, 0))
    out = [
        jax.ShapeDtypeStruct((size + PAD if carry else size, width), jnp.float32),
        jax.ShapeDtypeStruct((size, count), jnp.bfloat16),
        jax.ShapeDtypeStruct(state.shape, jnp.float32),
    ]
    if fresh:
        out.append(jax.ShapeDtypeStruct(rows.shape, jnp.bfloat16))
    args = [rows, block, state, source, target] + ([] if before is None else [before])
    whole = pl.BlockSpec(memory_space=pltpu.VMEM)
    return pl.pallas_call(
        functools.partial(meet_kernel, first, step, edges, fresh, carry),
        grid=(1,),
        out_shape=out,
        in_specs=[whole, spec] + [whole] * (len(args) - 2),
        out_specs=[whole] * len(out),
        cost_estimate=pl.CostEstimate(
            flops=4 * size * count * width, transcendentals=size * count, bytes_accessed=8 * size * width
        ),
        compiler_params=pltpu.CompilerParams(vmem_limit_bytes=24 << 20),
    )(*args)


def bucket_kernel(pieces, *refs):
    rows_ref, state_ref, through_ref, *refs = refs
    grads, blocks = refs[:pieces], refs[pieces : 2 * pieces]
    new_ref, new_state_ref, out_ref, *rounded = refs[2 * pieces :]
    rows_grad = 0.0
    for grad_ref, block_ref in zip(grads, blocks, strict=True):
        rows_grad = rows_grad + dot(grad_ref[...], block_ref[...].astype(jnp.bfloat16), ((0,), (0,)))
    total = state_ref.shape[1]
    mine = own_rows(0, total, total)
    state = jnp.sum(jnp.where(mine, state_ref[...], 0.0), axis=1, keepdims=True)
    state = state + jnp.mean(rows_grad * rows_grad, axis=1, keepdims=True)
    new = rows_ref[...] - rows_grad * (0.1 / jnp.sqrt(state))
    new_ref[...] = new
    if rounded:
        rounded[0][...] = new.astype(jnp.bfloat16)
    new_state_ref[...] = jnp.sum(jnp.where(mine, state, 0.0), axis=0, keepdims=True)
    out_ref[...] = through_ref[...]


def update_bucket(rows, state, through, grads, blocks, offsets, last):
    count, width = rows.shape
    out = [
        jax.ShapeDtypeStruct(rows.shape, jnp.float32),
        jax.ShapeDtypeStruct(state.shape, jnp.float32),
        jax.ShapeDtypeStruct(through.shape, jnp.float32),
    ]
    if not last:
        out.append(jax.ShapeDtypeStruct(rows.shape, jnp.bfloat16))
    whole = pl.BlockSpec(memory_space=pltpu.VMEM)
    specs = []
    for (_, size), offset in zip(CHUNKS, offsets, strict=True):
        if offset is None:
            specs.append(whole)
        else:
            specs.append(
                pl.BlockSpec((pl.Element(size), pl.Element(width)), functools.partial(lambda at, g: (at, 0), offset))
            )
    return pl.pallas_call(
        functools.partial(bucket_kernel, len(grads)),
        grid=(1,),
        out_shape=out,
        in_specs=[whole] * (3 + len(grads)) + specs,
        out_specs=[whole] * len(out),
        cost_estimate=pl.CostEstimate(
            flops=2 * count * count * width, transcendentals=count, bytes_accessed=12 * count * width
        ),
        compiler_params=pltpu.CompilerParams(vmem_limit_bytes=24 << 20),
    )(rows, state, through, *grads, *blocks)


def body(vertex, vertex_state, context, context_state, edge_source, edge_target):
    size = places()
    count = context.shape[0]
    rows, row_state = vertex, vertex_state.reshape(1, -1)
    rounded = vertex
    blocks, offsets = [context] * len(CHUNKS), [a for a, _ in CHUNKS]
    state = context_state.reshape(1, -1)
    for step in range(ROUNDS):
        last = step == ROUNDS - 1
        pairs = step_outer(*size) if last else step_inner(*size)
        moved, grads, states = [], [], None
        for k, (first, n) in enumerate(CHUNKS):
            new, grad, states, *more = meet(
                rounded, blocks[k], offsets[k], state, edge_source, edge_target, states, first, n, step, last
            )
            if more:
                rounded = more[0]
            grads.append(grad)
            moved.append(lax.ppermute(new, BOTH, pairs))
        rows, row_state, states, *more = update_bucket(rows, row_state, states, grads, blocks, offsets, last)
        blocks, offsets = moved, [None] * len(CHUNKS)
        if not last:
            rounded = more[0]
            state = lax.ppermute(states, BOTH, pairs)
    n = CHUNKS[-1][1]
    state = blocks[-1][n, :count]
    block = jnp.concatenate(blocks[:-1] + [blocks[-1][:n]])
    return rows, row_state.reshape(-1), block, state


def solution(mesh):
    flat, table = P(("outer", "inner")), P(("outer", "inner"), None)
    return jax.shard_map(
        body,
        mesh=mesh,
        in_specs=(table, flat, table, flat, table, table),
        out_specs=(table, flat, table, flat),
        check_vma=False,
    )
```

time: 150 us -> 150 us (level)
  waiting for transfers between devices: 118 us -> 109 us
  Pallas kernels: 0 us -> 7.65 us
  starting transfers between devices: 18.2 us -> 25 us
  matrix products: 6.51 us -> 0 us
  other arithmetic: 3.21 us -> 1.06 us
  local copies, waits for them, and re-layouts: 3.74 us -> 5.78 us
    ppermute x6 -> x8, waiting for transfers between devices: 118 us -> 109 us  [the longest x2 98.7 us: body(): state = lax.ppermute(states, BOTH, pairs)]
    pallas_call x0 -> x9, Pallas kernels: none -> 7.65 us  [the longest x6 4.75 us: meet(): pl.pallas_call(functools.partial(meet_kernel, first, step, edges, fresh,...]
    ppermute x6 -> x8, starting transfers between devices: 18.2 us -> 25 us  [the longest x6 18.3 us: body(): moved.append(lax.ppermute(new, BOTH, pairs))]
    dot_general x12 -> x0, matrix products: 6.51 us -> none  [the longest x3 2.69 us: gradient(): scores = jnp.dot(rows_b, block_b.T, preferred_element_type=jnp.float32)]
    sub x6 -> x0, other arithmetic: 2.6 us -> none  [adagrad(): return (weights - 0.1 * grad / jnp.sqrt(state)[:, None], state)]
    unnamed x12 -> x18, local copies, waits for them, and re-layouts: 3.02 us -> 5.19 us
  transfers between devices with their start and end apart: 6 -> 8, of which waited for: 3 -> 3; matrix products, arithmetic and copies ran while one was open for 4% -> 0% of each run, Pallas kernels for 0% -> 5%
where the time goes in v1:
time: 150 us
  waiting for transfers between devices  109 us (73%)
  starting transfers between devices  25 us (17%)
  Pallas kernels  7.65 us (5%)
  local copies, waits for them, and re-layouts  5.78 us (4%)
    ppermute x2, waiting for transfers between devices, body(): state = lax.ppermute(states, BOTH, pairs)  98.7 us
    ppermute x6, starting transfers between devices, body(): moved.append(lax.ppermute(new, BOTH, pairs))  18.3 us
    ppermute x6, waiting for transfers between devices, body(): moved.append(lax.ppermute(new, BOTH, pairs))  10.8 us
    ppermute x2, starting transfers between devices, body(): state = lax.ppermute(states, BOTH, pairs)  6.73 us
    unnamed x18, local copies, waits for them, and re-layouts  5.19 us
    pallas_call x6, Pallas kernels, meet(): pl.pallas_call(functools.partial(meet_kernel, first, step, edges, fresh,...  4.75 us
  transfers between devices with their start and end apart: 8, of which 3 were waited for; matrix products, arithmetic and copies ran while one was open for 0% of the time, Pallas kernels for 5%

profile of v1, /device:TPU:56, one launch (start us, length us, event | category | flops | bytes accessed | tf_op | source)
XLA Modules:
  0.0 149.7 jit_solution(5945910837695351282)
XLA Ops:
  0.6 0.0 copy-start.7
  0.6 0.7 copy-done.7
  1.3 0.0 copy-start
  1.3 1.2 copy-done
  2.5 0.0 copy-start.2
  2.5 1.2 copy-done.2
  3.8 0.0 copy-start.3
  3.8 0.7 copy-done.3
  4.5 0.0 copy-start.5
  4.5 0.7 copy-done.5
  5.1 0.0 copy-start.1
  5.1 0.0 copy-start.4
  5.2 0.0 copy-start.6
  5.2 0.8 shard_map.93
  6.0 4.5 %collective-permute-start.2 = (f32[144,1024]{1,0:T(8,128)S(1)}, f32[144,1024]{1,0:T(8,128)S(1)}, u32[]{:S(2)}, u32[]{:S(2)}) collective-permute-start(f32[144,1024]{1,0:T(8,128)S(1)} %get-tuple-element.43), channel_id=1, source_target_pairs={{0,1},{1,2},{2,3},{3,4},{4,5},{5,6},{6,7},{7,8},{8,9},{9,10},{10,1... | collective-permute-start | bytes 1769480 | tf_op jit(solution)/shard_map/ppermute | solution.py:172
  10.5 0.0 copy-done.1
  10.5 0.0 copy-done.4
  10.5 0.0 copy-done.6
  10.5 0.8 shard_map.94
  11.3 4.5 %collective-permute-start = (f32[112,1024]{1,0:T(8,128)S(1)}, f32[112,1024]{1,0:T(8,128)S(1)}, u32[]{:S(2)}, u32[]{:S(2)}) collective-permute-start(f32[112,1024]{1,0:T(8,128)S(1)} %get-tuple-element.41), channel_id=1, source_target_pairs={{0,1},{1,2},{2,3},{3,4},{4,5},{5,6},{6,7},{7,8},{8,9},{9,10},{10,1... | collective-permute-start | bytes 1376264 | tf_op jit(solution)/shard_map/ppermute | solution.py:172
  15.8 0.0 copy-start.8
  15.8 0.7 copy-done.8
  16.5 0.6 shard_map.95
  17.1 4.8 %collective-permute-start.1 = (f32[1,256]{1,0:T(1,128)S(1)}, f32[1,256]{1,0:T(1,128)S(1)}, u32[]{:S(2)}, u32[]{:S(2)}) collective-permute-start(f32[1,256]{1,0:T(1,128)S(1)} %get-tuple-element.42), channel_id=1, source_target_pairs={{0,1},{1,2},{2,3},{3,4},{4,5},{5,6},{6,7},{7,8},{8,9},{9,10},{10,1... | collective-permute-start | bytes 3080 | tf_op jit(solution)/shard_map/ppermute | solution.py:177
  21.9 67.0 %collective-permute-done.1.refs_2_ = f32[1,256]{1,0:T(1,128)S(1)} collective-permute-done((f32[1,256]{1,0:T(1,128)S(1)}, f32[1,256]{1,0:T(1,128)S(1)}, u32[]{:S(2)}, u32[]{:S(2)}) %collective-permute-start.1) | collective-permute-done | bytes 1056 | tf_op jit(solution)/shard_map/ppermute | solution.py:177
  88.9 0.0 collective-permute-done.2.refs_1_.refs_5_
  88.9 0.8 shard_map.96
  89.7 1.9 %collective-permute-start.5 = (f32[144,1024]{1,0:T(8,128)S(1)}, f32[144,1024]{1,0:T(8,128)S(1)}, u32[]{:S(2)}, u32[]{:S(2)}) collective-permute-start(f32[144,1024]{1,0:T(8,128)S(1)} %get-tuple-element.53), channel_id=1, source_target_pairs={{0,1},{1,2},{2,3},{3,4},{4,5},{5,6},{6,7},{7,8},{8,9},{9,10},{10,1... | collective-permute-start | bytes 1769480 | tf_op jit(solution)/shard_map/ppermute | solution.py:172
  91.7 0.0 collective-permute-done.refs_1_.refs_6_
  91.7 0.8 shard_map.97
  92.5 1.9 %collective-permute-start.3 = (f32[112,1024]{1,0:T(8,128)S(1)}, f32[112,1024]{1,0:T(8,128)S(1)}, u32[]{:S(2)}, u32[]{:S(2)}) collective-permute-start(f32[112,1024]{1,0:T(8,128)S(1)} %get-tuple-element.51), channel_id=1, source_target_pairs={{0,1},{1,2},{2,3},{3,4},{4,5},{5,6},{6,7},{7,8},{8,9},{9,10},{10,1... | collective-permute-start | bytes 1376264 | tf_op jit(solution)/shard_map/ppermute | solution.py:172
  94.4 0.7 shard_map.98
  95.1 1.9 %collective-permute-start.4 = (f32[1,256]{1,0:T(1,128)S(1)}, f32[1,256]{1,0:T(1,128)S(1)}, u32[]{:S(2)}, u32[]{:S(2)}) collective-permute-start(f32[1,256]{1,0:T(1,128)S(1)} %get-tuple-element.52), channel_id=1, source_target_pairs={{0,1},{1,2},{2,3},{3,4},{4,5},{5,6},{6,7},{7,8},{8,9},{9,10},{10,1... | collective-permute-start | bytes 3080 | tf_op jit(solution)/shard_map/ppermute | solution.py:177
  97.0 31.7 %collective-permute-done.4.refs_2_ = f32[1,256]{1,0:T(1,128)S(1)} collective-permute-done((f32[1,256]{1,0:T(1,128)S(1)}, f32[1,256]{1,0:T(1,128)S(1)}, u32[]{:S(2)}, u32[]{:S(2)}) %collective-permute-start.4) | collective-permute-done | bytes 1056 | tf_op jit(solution)/shard_map/ppermute | solution.py:177
  128.7 0.0 collective-permute-done.5.refs_1_.refs_5_
  128.7 0.8 shard_map.99
  129.5 1.9 %collective-permute-start.6 = (f32[144,1024]{1,0:T(8,128)S(1)}, f32[144,1024]{1,0:T(8,128)S(1)}, u32[]{:S(2)}, u32[]{:S(2)}) collective-permute-start(f32[144,1024]{1,0:T(8,128)S(1)} %get-tuple-element.60), channel_id=1, source_target_pairs={{0,48},{1,49},{2,50},{3,51},{4,52},{5,53},{6,54},{7,55},{8,56},{9,... | collective-permute-start | bytes 1769480 | tf_op jit(solution)/shard_map/ppermute | solution.py:172
  131.4 0.0 collective-permute-done.3.refs_1_.refs_6_
  131.4 0.8 shard_map.100
  132.2 3.5 %collective-permute-start.7 = (f32[120,1024]{1,0:T(8,128)S(1)}, f32[120,1024]{1,0:T(8,128)S(1)}, u32[]{:S(2)}, u32[]{:S(2)}) collective-permute-start(f32[120,1024]{1,0:T(8,128)S(1)} %get-tuple-element.61), channel_id=1, source_target_pairs={{0,48},{1,49},{2,50},{3,51},{4,52},{5,53},{6,54},{7,55},{8,56},{9,... | collective-permute-start | bytes 1474568 | tf_op jit(solution)/shard_map/ppermute | solution.py:172
  135.7 1.6 %shard_map.101 = (f32[256,1024]{1,0:T(8,128)}, f32[1,256]{1,0:T(1,128)}, f32[1,256]{1,0:T(1,128)}) custom-call(f32[256,1024]{1,0:T(8,128)S(1)} %get-tuple-element.48.refs_0_, f32[1,256]{1,0:T(1,128)S(1)} %get-tuple-element.49.refs_1_, f32[1,256]{1,0:T(1,128)S(1)} %get-tuple-element.55.refs_2_, bf16[144,256]{1,0:T(8,128)(2,1)S(1)} %get-tuple-element.56.refs_3_, ...), custom_call_target="tpu_custom_call" | custom-call | flops 134217728 | bytes 3145728 | tf_op jit(solution)/shard_map/pallas_call | solution.py:141
  137.3 10.7 %collective-permute-done.7 = f32[120,1024]{1,0:T(8,128)S(1)} collective-permute-done((f32[120,1024]{1,0:T(8,128)S(1)}, f32[120,1024]{1,0:T(8,128)S(1)}, u32[]{:S(2)}, u32[]{:S(2)}) %collective-permute-start.7) | collective-permute-done | bytes 491552 | tf_op jit(solution)/shard_map/ppermute | solution.py:172
  148.1 0.6 slice.9
  148.7 0.0 collective-permute-done.6
  148.7 1.1 pad_maximum_fusion
  (1 shorter events, 0.0 us)
Async XLA Ops:
  0.6 0.7 copy-start.7
  1.3 1.2 copy-start
  2.5 1.2 copy-start.2
  3.8 0.7 copy-start.3
  4.5 0.7 copy-start.5
  5.1 5.3 %copy-start.1 = (f32[256,1024]{1,0:T(8,128)S(1)}, f32[256,1024]{1,0:T(8,128)}, u32[]{:S(2)}) copy-start(f32[256,1024]{1,0:T(8,128)} %refs_6_.1) | copy-start | bytes 3145732
  5.1 5.3 %copy-start.4 = (s32[1,1536]{1,0:T(1,128)S(1)}, s32[1,1536]{1,0:T(1,128)}, u32[]{:S(2)}) copy-start(s32[1,1536]{1,0:T(1,128)} %refs_3_.11) | copy-start | bytes 18436
  5.2 5.3 %copy-start.6 = (s32[1,1536]{1,0:T(1,128)S(1)}, s32[1,1536]{1,0:T(1,128)}, u32[]{:S(2)}) copy-start(s32[1,1536]{1,0:T(1,128)} %refs_4_.11) | copy-start | bytes 18436
  6.0 83.0 %collective-permute-start.2 = (f32[144,1024]{1,0:T(8,128)S(1)}, f32[144,1024]{1,0:T(8,128)S(1)}, u32[]{:S(2)}, u32[]{:S(2)}) collective-permute-start(f32[144,1024]{1,0:T(8,128)S(1)} %get-tuple-element.43), channel_id=1, source_target_pairs={{0,1},{1,2},{2,3},{3,4},{4,5},{5,6},{6,7},{7,8},{8,9},{9,10},{10,1... | collective-permute-start | bytes 1769480 | tf_op jit(solution)/shard_map/ppermute | solution.py:172
  11.3 80.4 %collective-permute-start = (f32[112,1024]{1,0:T(8,128)S(1)}, f32[112,1024]{1,0:T(8,128)S(1)}, u32[]{:S(2)}, u32[]{:S(2)}) collective-permute-start(f32[112,1024]{1,0:T(8,128)S(1)} %get-tuple-element.41), channel_id=1, source_target_pairs={{0,1},{1,2},{2,3},{3,4},{4,5},{5,6},{6,7},{7,8},{8,9},{9,10},{10,1... | collective-permute-start | bytes 1376264 | tf_op jit(solution)/shard_map/ppermute | solution.py:172
  15.8 0.7 copy-start.8
  17.1 71.8 %collective-permute-start.1 = (f32[1,256]{1,0:T(1,128)S(1)}, f32[1,256]{1,0:T(1,128)S(1)}, u32[]{:S(2)}, u32[]{:S(2)}) collective-permute-start(f32[1,256]{1,0:T(1,128)S(1)} %get-tuple-element.42), channel_id=1, source_target_pairs={{0,1},{1,2},{2,3},{3,4},{4,5},{5,6},{6,7},{7,8},{8,9},{9,10},{10,1... | collective-permute-start | bytes 3080 | tf_op jit(solution)/shard_map/ppermute | solution.py:177
  89.7 38.9 %collective-permute-start.5 = (f32[144,1024]{1,0:T(8,128)S(1)}, f32[144,1024]{1,0:T(8,128)S(1)}, u32[]{:S(2)}, u32[]{:S(2)}) collective-permute-start(f32[144,1024]{1,0:T(8,128)S(1)} %get-tuple-element.53), channel_id=1, source_target_pairs={{0,1},{1,2},{2,3},{3,4},{4,5},{5,6},{6,7},{7,8},{8,9},{9,10},{10,1... | collective-permute-start | bytes 1769480 | tf_op jit(solution)/shard_map/ppermute | solution.py:172
  92.5 39.0 %collective-permute-start.3 = (f32[112,1024]{1,0:T(8,128)S(1)}, f32[112,1024]{1,0:T(8,128)S(1)}, u32[]{:S(2)}, u32[]{:S(2)}) collective-permute-start(f32[112,1024]{1,0:T(8,128)S(1)} %get-tuple-element.51), channel_id=1, source_target_pairs={{0,1},{1,2},{2,3},{3,4},{4,5},{5,6},{6,7},{7,8},{8,9},{9,10},{10,1... | collective-permute-start | bytes 1376264 | tf_op jit(solution)/shard_map/ppermute | solution.py:172
  95.1 33.6 %collective-permute-start.4 = (f32[1,256]{1,0:T(1,128)S(1)}, f32[1,256]{1,0:T(1,128)S(1)}, u32[]{:S(2)}, u32[]{:S(2)}) collective-permute-start(f32[1,256]{1,0:T(1,128)S(1)} %get-tuple-element.52), channel_id=1, source_target_pairs={{0,1},{1,2},{2,3},{3,4},{4,5},{5,6},{6,7},{7,8},{8,9},{9,10},{10,1... | collective-permute-start | bytes 3080 | tf_op jit(solution)/shard_map/ppermute | solution.py:177
  129.5 19.2 %collective-permute-start.6 = (f32[144,1024]{1,0:T(8,128)S(1)}, f32[144,1024]{1,0:T(8,128)S(1)}, u32[]{:S(2)}, u32[]{:S(2)}) collective-permute-start(f32[144,1024]{1,0:T(8,128)S(1)} %get-tuple-element.60), channel_id=1, source_target_pairs={{0,48},{1,49},{2,50},{3,51},{4,52},{5,53},{6,54},{7,55},{8,56},{9,... | collective-permute-start | bytes 1769480 | tf_op jit(solution)/shard_map/ppermute | solution.py:172
  132.2 15.8 %collective-permute-start.7 = (f32[120,1024]{1,0:T(8,128)S(1)}, f32[120,1024]{1,0:T(8,128)S(1)}, u32[]{:S(2)}, u32[]{:S(2)}) collective-permute-start(f32[120,1024]{1,0:T(8,128)S(1)} %get-tuple-element.61), channel_id=1, source_target_pairs={{0,48},{1,49},{2,50},{3,51},{4,52},{5,53},{6,54},{7,55},{8,56},{9,... | collective-permute-start | bytes 1474568 | tf_op jit(solution)/shard_map/ppermute | solution.py:172

commit v2 on v1

v2 whole, which is shorter than its diff:
```python
import functools

import jax
import jax.numpy as jnp
from jax import lax
from jax.experimental import pallas as pl
from jax.experimental.pallas import tpu as pltpu
from jax.sharding import PartitionSpec as P

ROUNDS = 3
BOTH = ("outer", "inner")
CHUNKS = ((0, 144), (144, 112))
PAD = 8
LIMIT = 40 << 20
HBM = pl.BlockSpec(memory_space=pltpu.HBM)
VMEM = pl.BlockSpec(memory_space=pltpu.VMEM)


def step_inner(n_outer, n_inner):
    return [(o * n_inner + i, o * n_inner + (i + 1) % n_inner) for o in range(n_outer) for i in range(n_inner)]


def step_outer(n_outer, n_inner):
    return [(o * n_inner + i, (o + 1) % n_outer * n_inner + i) for o in range(n_outer) for i in range(n_inner)]


def dot(a, b, contract):
    return lax.dot_general(a, b, (contract, ((), ())), preferred_element_type=jnp.float32)


def hot(index, first, size):
    number = lax.broadcasted_iota(jnp.int32, (size, index.shape[1]), 0) + first
    return jnp.where(number == index, 1.0, 0.0).astype(jnp.bfloat16)


def own_rows(first, size, total):
    row = lax.broadcasted_iota(jnp.int32, (size, total), 0) + first
    return row == lax.broadcasted_iota(jnp.int32, (size, total), 1)


def edge_counts(source_ref, target_ref, step, edges, first, size, count):
    window = pl.ds(step * edges, edges)
    return dot(hot(target_ref[:, window], first, size), hot(source_ref[:, window], 0, count), ((1,), (1,)))


def update_chunk(first, rows_b, block, state_row, counts, new_ref, grad_ref):
    size, total = block.shape[0], state_row.shape[1]
    prob = jax.nn.sigmoid(dot(block.astype(jnp.bfloat16), rows_b, ((1,), (1,))))
    grad = (prob / total - counts * (1.0 - prob)).astype(jnp.bfloat16)
    grad_ref[...] = grad
    block_grad = dot(grad, rows_b, ((1,), (0,)))
    mine = own_rows(first, size, total)
    state = jnp.sum(jnp.where(mine, state_row, 0.0), axis=1, keepdims=True)
    state = state + jnp.mean(block_grad * block_grad, axis=1, keepdims=True)
    new_ref[pl.ds(0, size), :] = block - block_grad * (0.1 / jnp.sqrt(state))
    new_ref[pl.ds(size, PAD), :] = jnp.zeros((PAD, new_ref.shape[1]), jnp.float32)
    new_ref[pl.ds(size, 1), pl.ds(0, total)] = jnp.sum(jnp.where(mine, state, 0.0), axis=0, keepdims=True)


def first_kernel(first, size, rows_hbm, block_hbm, state_hbm, source_hbm, target_hbm, *refs):
    outs, scratch = refs[:-6], refs[-6:]
    new_ref, grad_ref = outs[0], outs[1]
    rows_ref, block_ref, state_ref, source_ref, target_ref, sems = scratch
    pairs = [
        (source_hbm, source_ref),
        (target_hbm, target_ref),
        (state_hbm, state_ref),
        (rows_hbm, rows_ref),
        (block_hbm.at[pl.ds(first, size), :], block_ref),
    ]
    copies = [pltpu.make_async_copy(a, b, sems.at[k]) for k, (a, b) in enumerate(pairs)]
    for copy in copies:
        copy.start()
    for copy in copies[:3]:
        copy.wait()
    edges = source_ref.shape[1] // ROUNDS
    counts = edge_counts(source_ref, target_ref, 0, edges, first, size, rows_ref.shape[0])
    copies[3].wait()
    rows_b = rows_ref[...].astype(jnp.bfloat16)
    if len(outs) > 2:
        outs[2][...] = rows_b
    copies[4].wait()
    update_chunk(first, rows_b, block_ref[...], state_ref[...], counts, new_ref, grad_ref)


def chunk_outs(size, count, width):
    return [
        jax.ShapeDtypeStruct((size + PAD, width), jnp.float32),
        jax.ShapeDtypeStruct((size, count), jnp.bfloat16),
    ]


def chunk_cost(size, count, width):
    return pl.CostEstimate(
        flops=4 * size * count * width, transcendentals=size * count, bytes_accessed=8 * size * width
    )


def meet_first(rows, context, state, source, target, first, size):
    count, width = rows.shape
    out = chunk_outs(size, count, width)
    if rows.dtype == jnp.float32:
        out.append(jax.ShapeDtypeStruct(rows.shape, jnp.bfloat16))
    return pl.pallas_call(
        functools.partial(first_kernel, first, size),
        out_shape=out,
        in_specs=[HBM if rows.dtype == jnp.float32 else pl.BlockSpec(memory_space=pl.ANY)] + [HBM] * 4,
        out_specs=[VMEM] * len(out),
        scratch_shapes=[
            pltpu.VMEM(rows.shape, rows.dtype),
            pltpu.VMEM((size, width), jnp.float32),
            pltpu.VMEM(state.shape, jnp.float32),
            pltpu.VMEM(source.shape, jnp.int32),
            pltpu.VMEM(target.shape, jnp.int32),
            pltpu.SemaphoreType.DMA((5,)),
        ],
        cost_estimate=chunk_cost(size, count, width),
        compiler_params=pltpu.CompilerParams(vmem_limit_bytes=LIMIT),
    )(rows, context, state, source, target)


def meet_kernel(first, step, edges, rows_ref, block_ref, source_ref, target_ref, *refs):
    new_ref, grad_ref = refs[-2:]
    size, total = grad_ref.shape
    counts = edge_counts(source_ref, target_ref, step, edges, first, size, rows_ref.shape[0])
    state_row = block_ref[pl.ds(size, 1), pl.ds(0, total)]
    update_chunk(first, rows_ref[...], block_ref[pl.ds(0, size), :], state_row, counts, new_ref, grad_ref)


def meet(rows_b, block, source, target, after, first, size, step):
    count, width = rows_b.shape
    out = chunk_outs(size, count, width)
    return pl.pallas_call(
        functools.partial(meet_kernel, first, step, source.shape[1] // ROUNDS),
        out_shape=out,
        in_specs=[VMEM] * 4 + [pl.BlockSpec(memory_space=pl.ANY)] * len(after),
        out_specs=[VMEM] * len(out),
        cost_estimate=chunk_cost(size, count, width),
        compiler_params=pltpu.CompilerParams(vmem_limit_bytes=LIMIT),
    )(rows_b, block, source, target, *after)


def bucket_kernel(sizes, rows_ref, state_ref, *refs):
    pieces = len(sizes)
    grads, blocks = refs[:pieces], refs[pieces : 2 * pieces]
    new_ref, new_state_ref, *rounded = refs[2 * pieces :]
    rows_grad = 0.0
    for (first, size), grad_ref, block_ref in zip(sizes, grads, blocks, strict=True):
        block = block_ref[pl.ds(first, size), :].astype(jnp.bfloat16)
        rows_grad = rows_grad + dot(grad_ref[...], block, ((0,), (0,)))
    total = state_ref.shape[1]
    mine = own_rows(0, total, total)
    state = jnp.sum(jnp.where(mine, state_ref[...], 0.0), axis=1, keepdims=True)
    state = state + jnp.mean(rows_grad * rows_grad, axis=1, keepdims=True)
    new = rows_ref[...] - rows_grad * (0.1 / jnp.sqrt(state))
    new_ref[...] = new
    if rounded:
        rounded[0][...] = new.astype(jnp.bfloat16)
    new_state_ref[...] = jnp.sum(jnp.where(mine, state, 0.0), axis=0, keepdims=True)


def update_bucket(rows, state, grads, blocks, fresh, last):
    count, width = rows.shape
    out = [jax.ShapeDtypeStruct(rows.shape, jnp.float32), jax.ShapeDtypeStruct(state.shape, jnp.float32)]
    if not last:
        out.append(jax.ShapeDtypeStruct(rows.shape, jnp.bfloat16))
    sizes = [(first if fresh else 0, size) for first, size in CHUNKS]
    return pl.pallas_call(
        functools.partial(bucket_kernel, sizes),
        out_shape=out,
        in_specs=[VMEM] * (2 + 2 * len(grads)),
        out_specs=[VMEM] * len(out),
        cost_estimate=pl.CostEstimate(
            flops=2 * count * count * width, transcendentals=count, bytes_accessed=12 * count * width
        ),
        compiler_params=pltpu.CompilerParams(vmem_limit_bytes=LIMIT),
    )(rows, state, *grads, *blocks)


def join_kernel(*refs):
    blocks, (out_ref, state_ref) = refs[:-2], refs[-2:]
    total = state_ref.shape[1]
    states = 0.0
    for (first, size), block_ref in zip(CHUNKS, blocks, strict=True):
        out_ref[pl.ds(first, size), :] = block_ref[pl.ds(0, size), :]
        states = states + block_ref[pl.ds(size, 1), pl.ds(0, total)]
    state_ref[...] = states


def join(blocks, count, width):
    return pl.pallas_call(
        join_kernel,
        out_shape=[jax.ShapeDtypeStruct((count, width), jnp.float32), jax.ShapeDtypeStruct((1, count), jnp.float32)],
        in_specs=[VMEM] * len(blocks),
        out_specs=[VMEM] * 2,
        compiler_params=pltpu.CompilerParams(vmem_limit_bytes=LIMIT),
    )(*blocks)


def body(vertex, vertex_state, context, context_state, edge_source, edge_target):
    size = lax.axis_size("outer"), lax.axis_size("inner")
    count, width = context.shape
    pinned = [pltpu.with_memory_space_constraint(x, pltpu.HBM) for x in (vertex, context, context_state.reshape(1, -1), edge_source, edge_target)]
    rows, row_state, rows_b = vertex, vertex_state.reshape(1, -1), pinned[0]
    blocks = [context] * len(CHUNKS)
    state = context_state.reshape(1, -1)
    for step in range(ROUNDS):
        last = step == ROUNDS - 1
        pairs = step_outer(*size) if last else step_inner(*size)
        moved, grads = [], []
        for k, (first, n) in enumerate(CHUNKS):
            if step == 0:
                new, grad, *more = meet_first(rows_b, *pinned[1:], first, n)
                rows_b = more[0] if more else rows_b
            else:
                new, grad = meet(rows_b, blocks[k], edge_source, edge_target, grads[-1:], first, n, step)
            grads.append(grad)
            moved.append(lax.ppermute(new, BOTH, pairs))
        rows, row_state, *more = update_bucket(rows, row_state, grads, blocks, step == 0, last)
        rows_b = more[0] if more else None
        blocks = moved
    block, state = join(blocks, count, width)
    return rows, row_state.reshape(-1), block, state.reshape(-1)


def solution(mesh):
    flat, table = P(("outer", "inner")), P(("outer", "inner"), None)
    return jax.shard_map(
        body,
        mesh=mesh,
        in_specs=(table, flat, table, flat, table, table),
        out_specs=(table, flat, table, flat),
        check_vma=False,
    )
```

time: 150 us -> 130 us (0.87)
  waiting for transfers between devices: 109 us -> 99.3 us
  starting transfers between devices: 25 us -> 17.7 us
  local copies, waits for them, and re-layouts: 5.78 us -> 0.67 us
  Pallas kernels: 7.65 us -> 11.4 us
    ppermute x2 -> x0, waiting for transfers between devices: 98.7 us -> none  [body(): state = lax.ppermute(states, BOTH, pairs)]
    ppermute x6, waiting for transfers between devices: 10.8 us -> 99.3 us  [body(): moved.append(lax.ppermute(new, BOTH, pairs))]
    ppermute x2 -> x0, starting transfers between devices: 6.73 us -> none  [body(): state = lax.ppermute(states, BOTH, pairs)]
    unnamed x18 -> x10, local copies, waits for them, and re-layouts: 5.19 us -> 0.67 us
    pallas_call x9 -> x10, Pallas kernels: 7.65 us -> 11.4 us  [the longest x2 4.24 us: meet_first(): pl.pallas_call(functools.partial(first_kernel, first, size), out_shape=ou...]
  transfers between devices with their start and end apart: 8 -> 6, of which waited for: 3 -> 5; matrix products, arithmetic and copies ran while one was open for 0% -> 0% of each run, Pallas kernels for 5% -> 6%
where the time goes in v2:
time: 130 us
  waiting for transfers between devices  99.3 us (76%)
  starting transfers between devices  17.7 us (14%)
  Pallas kernels  11.4 us (9%)
    ppermute x6, waiting for transfers between devices, body(): moved.append(lax.ppermute(new, BOTH, pairs))  99.3 us
    ppermute x6, starting transfers between devices, body(): moved.append(lax.ppermute(new, BOTH, pairs))  17.7 us
    pallas_call x2, Pallas kernels, meet_first(): pl.pallas_call(functools.partial(first_kernel, first, size), out_shape=ou...  4.24 us
    pallas_call x4, Pallas kernels, meet(): pl.pallas_call(functools.partial(meet_kernel, first, step, source.shape[1...  3.2 us
    pallas_call x3, Pallas kernels, update_bucket(): pl.pallas_call(functools.partial(bucket_kernel, sizes), out_shape=out, in...  2.94 us
  transfers between devices with their start and end apart: 6, of which 5 were waited for; matrix products, arithmetic and copies ran while one was open for 0% of the time, Pallas kernels for 6%

profile of v2, /device:TPU:56, one launch (start us, length us, event | category | flops | bytes accessed | tf_op | source)
XLA Modules:
  0.0 130.0 jit_solution(15692663941852041829)
XLA Ops:
  0.6 0.0 copy-start.1
  0.6 2.4 %shard_map.93 = (f32[152,1024]{1,0:T(8,128)S(1)}, bf16[144,256]{1,0:T(8,128)(2,1)S(1)}, bf16[256,1024]{1,0:T(8,128)(2,1)S(1)}) custom-call(f32[256,1024]{1,0:T(8,128)} %rows_ref.1, f32[256,1024]{1,0:T(8,128)} %refs_3_.1, f32[1,256]{1,0:T(1,128)} %bitcast.5, s32[1,1536]{1,0:T(1,128)} %source_ref.7, s32[1,1536]{1,0:T(1,128)} %target_ref.7), custom_call_target="tpu_custom_call" | custom-call | flops 150994944 | bytes 1179648 | tf_op jit(solution)/shard_map/pallas_call | solution.py:104
  3.0 0.0 copy-start
  3.0 4.6 %collective-permute-start = (f32[152,1024]{1,0:T(8,128)S(1)}, f32[152,1024]{1,0:T(8,128)S(1)}, u32[]{:S(2)}, u32[]{:S(2)}) collective-permute-start(f32[152,1024]{1,0:T(8,128)S(1)} %get-tuple-element.33), channel_id=1, source_target_pairs={{0,1},{1,2},{2,3},{3,4},{4,5},{5,6},{6,7},{7,8},{8,9},{9,10},{10,1... | collective-permute-start | bytes 1867784 | tf_op jit(solution)/shard_map/ppermute | solution.py:218
  7.7 1.9 %shard_map.94 = (f32[120,1024]{1,0:T(8,128)S(1)}, bf16[112,256]{1,0:T(8,128)(2,1)S(1)}) custom-call(bf16[256,1024]{1,0:T(8,128)(2,1)S(1)} %get-tuple-element.28.rows_hbm, f32[256,1024]{1,0:T(8,128)} %refs_3_.1, f32[1,256]{1,0:T(1,128)} %bitcast.6, s32[1,1536]{1,0:T(1,128)} %source_ref.7, s32[1,1536]{1,0:T(1,128)} %target_ref.7), custom_call_target="tpu_custom_call" | custom-call | flops 117440512 | bytes 917504 | tf_op jit(solution)/shard_map/pallas_call | solution.py:104
  9.5 4.5 %collective-permute-start.1 = (f32[120,1024]{1,0:T(8,128)S(1)}, f32[120,1024]{1,0:T(8,128)S(1)}, u32[]{:S(2)}, u32[]{:S(2)}) collective-permute-start(f32[120,1024]{1,0:T(8,128)S(1)} %get-tuple-element.35), channel_id=1, source_target_pairs={{0,1},{1,2},{2,3},{3,4},{4,5},{5,6},{6,7},{7,8},{8,9},{9,10},{10,1... | collective-permute-start | bytes 1474568 | tf_op jit(solution)/shard_map/ppermute | solution.py:218
  14.1 0.0 copy-start.4
  14.1 0.0 copy-done.1
  14.1 0.0 copy-done
  14.1 0.7 copy-done.4
  14.7 0.0 copy-start.2
  14.7 0.0 copy-start.3
  14.7 0.7 shard_map.95
  15.4 31.4 %collective-permute-done.block_ref.refs_2_ = f32[152,1024]{1,0:T(8,128)S(1)} collective-permute-done((f32[152,1024]{1,0:T(8,128)S(1)}, f32[152,1024]{1,0:T(8,128)S(1)}, u32[]{:S(2)}, u32[]{:S(2)}) %collective-permute-start) | collective-permute-done | bytes 622624 | tf_op jit(solution)/shard_map/ppermute | solution.py:218
  46.9 0.0 copy-done.2
  46.9 0.0 copy-done.3
  46.9 0.8 shard_map.96
  47.7 1.9 %collective-permute-start.2 = (f32[152,1024]{1,0:T(8,128)S(1)}, f32[152,1024]{1,0:T(8,128)S(1)}, u32[]{:S(2)}, u32[]{:S(2)}) collective-permute-start(f32[152,1024]{1,0:T(8,128)S(1)} %get-tuple-element.40), channel_id=1, source_target_pairs={{0,1},{1,2},{2,3},{3,4},{4,5},{5,6},{6,7},{7,8},{8,9},{9,10},{10,1... | collective-permute-start | bytes 1867784 | tf_op jit(solution)/shard_map/ppermute | solution.py:218
  49.6 18.1 %collective-permute-done.1.block_ref.refs_3_ = f32[120,1024]{1,0:T(8,128)S(1)} collective-permute-done((f32[120,1024]{1,0:T(8,128)S(1)}, f32[120,1024]{1,0:T(8,128)S(1)}, u32[]{:S(2)}, u32[]{:S(2)}) %collective-permute-start.1) | collective-permute-done | bytes 491552 | tf_op jit(solution)/shard_map/ppermute | solution.py:218
  67.7 0.8 shard_map.97
  68.5 2.9 %collective-permute-start.3 = (f32[120,1024]{1,0:T(8,128)S(1)}, f32[120,1024]{1,0:T(8,128)S(1)}, u32[]{:S(2)}, u32[]{:S(2)}) collective-permute-start(f32[120,1024]{1,0:T(8,128)S(1)} %get-tuple-element.42), channel_id=1, source_target_pairs={{0,1},{1,2},{2,3},{3,4},{4,5},{5,6},{6,7},{7,8},{8,9},{9,10},{10,1... | collective-permute-start | bytes 1474568 | tf_op jit(solution)/shard_map/ppermute | solution.py:218
  71.3 0.7 shard_map.98
  72.0 22.0 %collective-permute-done.2.block_ref.refs_2_ = f32[152,1024]{1,0:T(8,128)S(1)} collective-permute-done((f32[152,1024]{1,0:T(8,128)S(1)}, f32[152,1024]{1,0:T(8,128)S(1)}, u32[]{:S(2)}, u32[]{:S(2)}) %collective-permute-start.2) | collective-permute-done | bytes 622624 | tf_op jit(solution)/shard_map/ppermute | solution.py:218
  94.0 0.8 shard_map.99
  94.9 1.9 %collective-permute-start.4 = (f32[152,1024]{1,0:T(8,128)S(1)}, f32[152,1024]{1,0:T(8,128)S(1)}, u32[]{:S(2)}, u32[]{:S(2)}) collective-permute-start(f32[152,1024]{1,0:T(8,128)S(1)} %get-tuple-element.46), channel_id=1, source_target_pairs={{0,48},{1,49},{2,50},{3,51},{4,52},{5,53},{6,54},{7,55},{8,56},{9,... | collective-permute-start | bytes 1867784 | tf_op jit(solution)/shard_map/ppermute | solution.py:218
  96.8 16.9 %collective-permute-done.3.block_ref.refs_3_ = f32[120,1024]{1,0:T(8,128)S(1)} collective-permute-done((f32[120,1024]{1,0:T(8,128)S(1)}, f32[120,1024]{1,0:T(8,128)S(1)}, u32[]{:S(2)}, u32[]{:S(2)}) %collective-permute-start.3) | collective-permute-done | bytes 491552 | tf_op jit(solution)/shard_map/ppermute | solution.py:218
  113.7 0.8 shard_map.100
  114.5 1.9 %collective-permute-start.5 = (f32[120,1024]{1,0:T(8,128)S(1)}, f32[120,1024]{1,0:T(8,128)S(1)}, u32[]{:S(2)}, u32[]{:S(2)}) collective-permute-start(f32[120,1024]{1,0:T(8,128)S(1)} %get-tuple-element.47), channel_id=1, source_target_pairs={{0,48},{1,49},{2,50},{3,51},{4,52},{5,53},{6,54},{7,55},{8,56},{9,... | collective-permute-start | bytes 1474568 | tf_op jit(solution)/shard_map/ppermute | solution.py:218
  116.4 1.6 %shard_map.101 = (f32[256,1024]{1,0:T(8,128)}, f32[1,256]{1,0:T(1,128)}) custom-call(f32[256,1024]{1,0:T(8,128)S(1)} %get-tuple-element.37.rows_ref, f32[1,256]{1,0:T(1,128)S(1)} %get-tuple-element.38.state_ref, bf16[144,256]{1,0:T(8,128)(2,1)S(1)} %get-tuple-element.41.refs_0_, bf16[112,256]{1,0:T(8,128)(2,1)S(1)} %get-tuple-element.43.refs_1_, ...), custom_call_target="tpu_custom_call" | custom-call | flops 134217728 | bytes 3145728 | tf_op jit(solution)/shard_map/pallas_call | solution.py:168
  118.1 10.9 %collective-permute-done.5.refs_1_ = f32[120,1024]{1,0:T(8,128)S(1)} collective-permute-done((f32[120,1024]{1,0:T(8,128)S(1)}, f32[120,1024]{1,0:T(8,128)S(1)}, u32[]{:S(2)}, u32[]{:S(2)}) %collective-permute-start.5) | collective-permute-done | bytes 491552 | tf_op jit(solution)/shard_map/ppermute | solution.py:218
  128.9 0.0 collective-permute-done.4.refs_0_
  128.9 1.0 shard_map.102
Async XLA Ops:
  0.6 13.4 %copy-start.1 = (f32[256,1024]{1,0:T(8,128)S(1)}, f32[256,1024]{1,0:T(8,128)}, u32[]{:S(2)}) copy-start(f32[256,1024]{1,0:T(8,128)} %rows_ref.1) | copy-start | bytes 3145732
  3.0 11.1 %copy-start = (f32[256,1024]{1,0:T(8,128)S(1)}, f32[256,1024]{1,0:T(8,128)}, u32[]{:S(2)}) copy-start(f32[256,1024]{1,0:T(8,128)} %refs_3_.1) | copy-start | bytes 3145732
  3.0 43.8 %collective-permute-start = (f32[152,1024]{1,0:T(8,128)S(1)}, f32[152,1024]{1,0:T(8,128)S(1)}, u32[]{:S(2)}, u32[]{:S(2)}) collective-permute-start(f32[152,1024]{1,0:T(8,128)S(1)} %get-tuple-element.33), channel_id=1, source_target_pairs={{0,1},{1,2},{2,3},{3,4},{4,5},{5,6},{6,7},{7,8},{8,9},{9,10},{10,1... | collective-permute-start | bytes 1867784 | tf_op jit(solution)/shard_map/ppermute | solution.py:218
  9.5 58.1 %collective-permute-start.1 = (f32[120,1024]{1,0:T(8,128)S(1)}, f32[120,1024]{1,0:T(8,128)S(1)}, u32[]{:S(2)}, u32[]{:S(2)}) collective-permute-start(f32[120,1024]{1,0:T(8,128)S(1)} %get-tuple-element.35), channel_id=1, source_target_pairs={{0,1},{1,2},{2,3},{3,4},{4,5},{5,6},{6,7},{7,8},{8,9},{9,10},{10,1... | collective-permute-start | bytes 1474568 | tf_op jit(solution)/shard_map/ppermute | solution.py:218
  14.1 0.7 copy-start.4
  14.7 32.1 %copy-start.2 = (s32[1,1536]{1,0:T(1,128)S(1)}, s32[1,1536]{1,0:T(1,128)}, u32[]{:S(2)}) copy-start(s32[1,1536]{1,0:T(1,128)} %source_ref.7) | copy-start | bytes 18436
  14.7 32.1 %copy-start.3 = (s32[1,1536]{1,0:T(1,128)S(1)}, s32[1,1536]{1,0:T(1,128)}, u32[]{:S(2)}) copy-start(s32[1,1536]{1,0:T(1,128)} %target_ref.7) | copy-start | bytes 18436
  47.7 46.4 %collective-permute-start.2 = (f32[152,1024]{1,0:T(8,128)S(1)}, f32[152,1024]{1,0:T(8,128)S(1)}, u32[]{:S(2)}, u32[]{:S(2)}) collective-permute-start(f32[152,1024]{1,0:T(8,128)S(1)} %get-tuple-element.40), channel_id=1, source_target_pairs={{0,1},{1,2},{2,3},{3,4},{4,5},{5,6},{6,7},{7,8},{8,9},{9,10},{10,1... | collective-permute-start | bytes 1867784 | tf_op jit(solution)/shard_map/ppermute | solution.py:218
  68.5 45.2 %collective-permute-start.3 = (f32[120,1024]{1,0:T(8,128)S(1)}, f32[120,1024]{1,0:T(8,128)S(1)}, u32[]{:S(2)}, u32[]{:S(2)}) collective-permute-start(f32[120,1024]{1,0:T(8,128)S(1)} %get-tuple-element.42), channel_id=1, source_target_pairs={{0,1},{1,2},{2,3},{3,4},{4,5},{5,6},{6,7},{7,8},{8,9},{9,10},{10,1... | collective-permute-start | bytes 1474568 | tf_op jit(solution)/shard_map/ppermute | solution.py:218
  94.9 34.1 %collective-permute-start.4 = (f32[152,1024]{1,0:T(8,128)S(1)}, f32[152,1024]{1,0:T(8,128)S(1)}, u32[]{:S(2)}, u32[]{:S(2)}) collective-permute-start(f32[152,1024]{1,0:T(8,128)S(1)} %get-tuple-element.46), channel_id=1, source_target_pairs={{0,48},{1,49},{2,50},{3,51},{4,52},{5,53},{6,54},{7,55},{8,56},{9,... | collective-permute-start | bytes 1867784 | tf_op jit(solution)/shard_map/ppermute | solution.py:218
  114.5 14.4 %collective-permute-start.5 = (f32[120,1024]{1,0:T(8,128)S(1)}, f32[120,1024]{1,0:T(8,128)S(1)}, u32[]{:S(2)}, u32[]{:S(2)}) collective-permute-start(f32[120,1024]{1,0:T(8,128)S(1)} %get-tuple-element.47), channel_id=1, source_target_pairs={{0,48},{1,49},{2,50},{3,51},{4,52},{5,53},{6,54},{7,55},{8,56},{9,... | collective-permute-start | bytes 1474568 | tf_op jit(solution)/shard_map/ppermute | solution.py:218

commit v3 on v2

--- a/solution.py
+++ b/solution.py
@@ -9,8 +9,12 @@
 
 ROUNDS = 3
 BOTH = ("outer", "inner")
-CHUNKS = ((0, 144), (144, 112))
-PAD = 8
+Y_HI, Y_LO = 4, 2
+LANES = 128
+STATES = 8
+CHUNKS = ((0, 56, False, True), (56, 56, True, False), (112, 72, False, False), (184, 72, False, False))
+ORDERS = ((1, 0, 2, 3), (0, 2, 3, 1), (2, 3, 1, 0))
+RELAYS = {(1, 2): ((0, 1),), (1, 1): ((1, 0),)}
 LIMIT = 40 << 20
 HBM = pl.BlockSpec(memory_space=pltpu.HBM)
 VMEM = pl.BlockSpec(memory_space=pltpu.VMEM)
@@ -24,6 +28,16 @@
     return [(o * n_inner + i, (o + 1) % n_outer * n_inner + i) for o in range(n_outer) for i in range(n_inner)]
 
 
+def halfway(n_outer, n_inner):
+    share = n_outer // Y_LO
+    pairs = []
+    for o in range(n_outer):
+        for i in range(n_inner):
+            y = (i % Y_HI * Y_LO + o // share - 3) % (Y_HI * Y_LO)
+            pairs.append((o * n_inner + i, (y % Y_LO * share + o % share) * n_inner + i - i % Y_HI + y // Y_LO))
+    return pairs
+
+
 def dot(a, b, contract):
     return lax.dot_general(a, b, (contract, ((), ())), preferred_element_type=jnp.float32)
 
@@ -41,6 +55,16 @@
 def edge_counts(source_ref, target_ref, step, edges, first, size, count):
     window = pl.ds(step * edges, edges)
     return dot(hot(target_ref[:, window], first, size), hot(source_ref[:, window], 0, count), ((1,), (1,)))
+
+
+def unpack(ref, size):
+    parts = (ref.shape[0] - STATES) // size
+    return jnp.concatenate([ref[pl.ds(k * size, size), :] for k in range(parts)], axis=1)
+
+
+def unpack_states(ref, total):
+    at = ref.shape[0] - STATES
+    return jnp.concatenate([ref[pl.ds(at + k, 1), :] for k in range(total // LANES)], axis=1)
 
 
 def update_chunk(first, rows_b, block, state_row, counts, new_ref, grad_ref):
@@ -52,9 +76,14 @@
     mine = own_rows(first, size, total)
     state = jnp.sum(jnp.where(mine, state_row, 0.0), axis=1, keepdims=True)
     state = state + jnp.mean(block_grad * block_grad, axis=1, keepdims=True)
-    new_ref[pl.ds(0, size), :] = block - block_grad * (0.1 / jnp.sqrt(state))
-    new_ref[pl.ds(size, PAD), :] = jnp.zeros((PAD, new_ref.shape[1]), jnp.float32)
-    new_ref[pl.ds(size, 1), pl.ds(0, total)] = jnp.sum(jnp.where(mine, state, 0.0), axis=0, keepdims=True)
+    new = block - block_grad * (0.1 / jnp.sqrt(state))
+    states = jnp.sum(jnp.where(mine, state, 0.0), axis=0, keepdims=True)
+    parts = block.shape[1] // LANES
+    for k in range(parts):
+        new_ref[pl.ds(k * size, size), :] = new[:, k * LANES : (k + 1) * LANES]
+    new_ref[pl.ds(parts * size, STATES), :] = jnp.zeros((STATES, LANES), jnp.float32)
+    for k in range(total // LANES):
+        new_ref[pl.ds(parts * size + k, 1), :] = states[:, k * LANES : (k + 1) * LANES]
 
 
 def first_kernel(first, size, rows_hbm, block_hbm, state_hbm, source_hbm, target_hbm, *refs):
@@ -85,7 +114,7 @@
 
 def chunk_outs(size, count, width):
     return [
-        jax.ShapeDtypeStruct((size + PAD, width), jnp.float32),
+        jax.ShapeDtypeStruct((size * width // LANES + STATES, LANES), jnp.float32),
         jax.ShapeDtypeStruct((size, count), jnp.bfloat16),
     ]
 
@@ -121,10 +150,10 @@
 
 def meet_kernel(first, step, edges, rows_ref, block_ref, source_ref, target_ref, *refs):
     new_ref, grad_ref = refs[-2:]
-    size, total = grad_ref.shape
+    size = grad_ref.shape[0]
     counts = edge_counts(source_ref, target_ref, step, edges, first, size, rows_ref.shape[0])
-    state_row = block_ref[pl.ds(size, 1), pl.ds(0, total)]
-    update_chunk(first, rows_ref[...], block_ref[pl.ds(0, size), :], state_row, counts, new_ref, grad_ref)
+    state_row = unpack_states(block_ref, rows_ref.shape[0])
+    update_chunk(first, rows_ref[...], unpack(block_ref, size), state_row, counts, new_ref, grad_ref)
 
 
 def meet(rows_b, block, source, target, after, first, size, step):
@@ -140,14 +169,14 @@
     )(rows_b, block, source, target, *after)
 
 
-def bucket_kernel(sizes, rows_ref, state_ref, *refs):
-    pieces = len(sizes)
+def bucket_kernel(fresh, rows_ref, state_ref, *refs):
+    pieces = len(CHUNKS)
     grads, blocks = refs[:pieces], refs[pieces : 2 * pieces]
-    new_ref, new_state_ref, *rounded = refs[2 * pieces :]
+    new_ref, new_state_ref, *rounded = refs[-2:] if refs[-1].dtype == jnp.float32 else refs[-3:]
     rows_grad = 0.0
-    for (first, size), grad_ref, block_ref in zip(sizes, grads, blocks, strict=True):
-        block = block_ref[pl.ds(first, size), :].astype(jnp.bfloat16)
-        rows_grad = rows_grad + dot(grad_ref[...], block, ((0,), (0,)))
+    for (first, size, *_), grad_ref, block_ref in zip(CHUNKS, grads, blocks, strict=True):
+        block = block_ref[pl.ds(first, size), :] if fresh else unpack(block_ref, size)
+        rows_grad = rows_grad + dot(grad_ref[...], block.astype(jnp.bfloat16), ((0,), (0,)))
     total = state_ref.shape[1]
     mine = own_rows(0, total, total)
     state = jnp.sum(jnp.where(mine, state_ref[...], 0.0), axis=1, keepdims=True)
@@ -159,31 +188,30 @@
     new_state_ref[...] = jnp.sum(jnp.where(mine, state, 0.0), axis=0, keepdims=True)
 
 
-def update_bucket(rows, state, grads, blocks, fresh, last):
+def update_bucket(rows, state, grads, blocks, after, fresh, last):
     count, width = rows.shape
     out = [jax.ShapeDtypeStruct(rows.shape, jnp.float32), jax.ShapeDtypeStruct(state.shape, jnp.float32)]
     if not last:
         out.append(jax.ShapeDtypeStruct(rows.shape, jnp.bfloat16))
-    sizes = [(first if fresh else 0, size) for first, size in CHUNKS]
-    return pl.pallas_call(
-        functools.partial(bucket_kernel, sizes),
+    return pl.pallas_call(
+        functools.partial(bucket_kernel, fresh),
         out_shape=out,
-        in_specs=[VMEM] * (2 + 2 * len(grads)),
+        in_specs=[VMEM] * (2 + 2 * len(grads)) + [pl.BlockSpec(memory_space=pl.ANY)] * len(after),
         out_specs=[VMEM] * len(out),
         cost_estimate=pl.CostEstimate(
             flops=2 * count * count * width, transcendentals=count, bytes_accessed=12 * count * width
         ),
         compiler_params=pltpu.CompilerParams(vmem_limit_bytes=LIMIT),
-    )(rows, state, *grads, *blocks)
+    )(rows, state, *grads, *blocks, *after)
 
 
 def join_kernel(*refs):
     blocks, (out_ref, state_ref) = refs[:-2], refs[-2:]
     total = state_ref.shape[1]
     states = 0.0
-    for (first, size), block_ref in zip(CHUNKS, blocks, strict=True):
-        out_ref[pl.ds(first, size), :] = block_ref[pl.ds(0, size), :]
-        states = states + block_ref[pl.ds(size, 1), pl.ds(0, total)]
+    for (first, size, *_), block_ref in zip(CHUNKS, blocks, strict=True):
+        out_ref[pl.ds(first, size), :] = unpack(block_ref, size)
+        states = states + unpack_states(block_ref, total)
     state_ref[...] = states
 
 
@@ -198,27 +226,38 @@
 
 
 def body(vertex, vertex_state, context, context_state, edge_source, edge_target):
-    size = lax.axis_size("outer"), lax.axis_size("inner")
+    places = lax.axis_size("outer"), lax.axis_size("inner")
     count, width = context.shape
-    pinned = [pltpu.with_memory_space_constraint(x, pltpu.HBM) for x in (vertex, context, context_state.reshape(1, -1), edge_source, edge_target)]
-    rows, row_state, rows_b = vertex, vertex_state.reshape(1, -1), pinned[0]
+    direct, relays = step_inner(*places), dict(halfway(*places))
+    whole = [vertex, context, context_state.reshape(1, -1), edge_source, edge_target]
+    whole = [pltpu.with_memory_space_constraint(array, pltpu.HBM) for array in whole]
+    rows, row_state, rows_b = vertex, vertex_state.reshape(1, -1), whole[0]
     blocks = [context] * len(CHUNKS)
-    state = context_state.reshape(1, -1)
+    legs = {}
     for step in range(ROUNDS):
         last = step == ROUNDS - 1
-        pairs = step_outer(*size) if last else step_inner(*size)
-        moved, grads = [], []
-        for k, (first, n) in enumerate(CHUNKS):
+        moved, grads, previous = {}, {}, []
+        for k in ORDERS[step]:
+            first, size, *long_way = CHUNKS[k]
+            after = previous + [legs[at] for at in RELAYS.get((step, k), ())]
             if step == 0:
-                new, grad, *more = meet_first(rows_b, *pinned[1:], first, n)
+                new, grad, *more = meet_first(rows_b, *whole[1:], first, size)
                 rows_b = more[0] if more else rows_b
             else:
-                new, grad = meet(rows_b, blocks[k], edge_source, edge_target, grads[-1:], first, n, step)
-            grads.append(grad)
-            moved.append(lax.ppermute(new, BOTH, pairs))
-        rows, row_state, *more = update_bucket(rows, row_state, grads, blocks, step == 0, last)
+                new, grad = meet(rows_b, blocks[k], edge_source, edge_target, after, first, size, step)
+            previous, grads[k] = [grad], grad
+            if last:
+                moved[k] = lax.ppermute(new, BOTH, step_outer(*places))
+            elif long_way[step]:
+                legs[step, k] = lax.ppermute(new, BOTH, list(relays.items()))
+                moved[k] = lax.ppermute(legs[step, k], BOTH, [(relays[p], q) for p, q in direct])
+            else:
+                moved[k] = lax.ppermute(new, BOTH, direct)
+        after = [legs[at] for at in RELAYS.get((step, None), ())]
+        grads = [grads[k] for k in range(len(CHUNKS))]
+        rows, row_state, *more = update_bucket(rows, row_state, grads, blocks, after, step == 0, last)
         rows_b = more[0] if more else None
-        blocks = moved
+        blocks = [moved[k] for k in range(len(CHUNKS))]
     block, state = join(blocks, count, width)
     return rows, row_state.reshape(-1), block, state.reshape(-1)
 

time: 130 us -> 113 us (0.87)
  the two profiles are of different devices: /device:TPU:56 before, /device:TPU:8 now
where the time goes in v3:
time: 113 us; the launch traced here: 112 us
  waiting for transfers between devices  50.7 us (45%)
  starting transfers between devices  41.3 us (37%)
  Pallas kernels  18.5 us (16%)
    ppermute x6, waiting for transfers between devices, body(): moved[k] = lax.ppermute(new, BOTH, direct)  43 us
    ppermute x6, starting transfers between devices, body(): moved[k] = lax.ppermute(new, BOTH, direct)  19.7 us
    ppermute x4, starting transfers between devices, body(): moved[k] = lax.ppermute(new, BOTH, step_outer(*places))  9.25 us
    ppermute x2, starting transfers between devices, body(): legs[step, k] = lax.ppermute(new, BOTH, list(relays.items()))  7.97 us
    pallas_call x4, Pallas kernels, meet_first(): pl.pallas_call(functools.partial(first_kernel, first, size), out_shape=ou...  7.64 us
    pallas_call x8, Pallas kernels, meet(): pl.pallas_call(functools.partial(meet_kernel, first, step, source.shape[1...  6.1 us
    ppermute x4, waiting for transfers between devices, body(): moved[k] = lax.ppermute(new, BOTH, step_outer(*places))  4.68 us
    ppermute x2, starting transfers between devices, body(): lax.ppermute(legs[step, k], BOTH, [(relays[p], q) for p, q in direct])  4.42 us
  transfers between devices with their start and end apart: 14, of which 9 were waited for; matrix products, arithmetic and copies ran while one was open for 0% of the time, Pallas kernels for 14%

profile of v3, /device:TPU:8, one launch (start us, length us, event | category | flops | bytes accessed | tf_op | source)
XLA Modules:
  0.0 112.1 jit_solution(9871647829150885669)
XLA Ops:
  0.6 2.1 %shard_map.93 = (f32[456,128]{1,0:T(8,128)S(1)}, bf16[56,256]{1,0:T(8,128)(2,1)S(1)}, bf16[256,1024]{1,0:T(8,128)(2,1)S(1)}) custom-call(f32[256,1024]{1,0:T(8,128)} %rows_ref.1, f32[256,1024]{1,0:T(8,128)} %refs_7_.1, f32[1,256]{1,0:T(1,128)} %bitcast.5, s32[1,1536]{1,0:T(1,128)} %source_ref.15, s32[1,1536]{1,0:T(1,128)} %target_ref.15), custom_call_target="tpu_custom_call" | custom-call | flops 58720256 | bytes 458752 | tf_op jit(solution)/shard_map/pallas_call | solution.py:133
  2.8 6.0 %collective-permute-start.1 = (f32[456,128]{1,0:T(8,128)S(1)}, f32[456,128]{1,0:T(8,128)S(1)}, u32[]{:S(2)}, u32[]{:S(2)}) collective-permute-start(f32[456,128]{1,0:T(8,128)S(1)} %get-tuple-element.49), channel_id=1, source_target_pairs={{0,386},{1,387},{2,384},{3,385},{4,390},{5,391},{6,388},{7,389},{8... | collective-permute-start | bytes 700424 | tf_op jit(solution)/shard_map/ppermute | solution.py:252
  8.8 1.8 %shard_map.94 = (f32[456,128]{1,0:T(8,128)S(1)}, bf16[56,256]{1,0:T(8,128)(2,1)S(1)}) custom-call(bf16[256,1024]{1,0:T(8,128)(2,1)S(1)} %get-tuple-element.39.rows_hbm, f32[256,1024]{1,0:T(8,128)} %refs_7_.1, f32[1,256]{1,0:T(1,128)} %bitcast.6, s32[1,1536]{1,0:T(1,128)} %source_ref.15, s32[1,1536]{1,0:T(1,128)} %target_ref.15), custom_call_target="tpu_custom_call" | custom-call | flops 58720256 | bytes 458752 | tf_op jit(solution)/shard_map/pallas_call | solution.py:133
  10.6 9.6 %collective-permute-start = (f32[456,128]{1,0:T(8,128)S(1)}, f32[456,128]{1,0:T(8,128)S(1)}, u32[]{:S(2)}, u32[]{:S(2)}) collective-permute-start(f32[456,128]{1,0:T(8,128)S(1)} %get-tuple-element.47), channel_id=1, source_target_pairs={{0,1},{1,2},{2,3},{3,4},{4,5},{5,6},{6,7},{7,8},{8,9},{9,10},{10,1... | collective-permute-start | bytes 700424 | tf_op jit(solution)/shard_map/ppermute | solution.py:255
  20.2 0.0 copy-start.1
  20.2 1.9 %shard_map.95 = (f32[584,128]{1,0:T(8,128)S(1)}, bf16[72,256]{1,0:T(8,128)(2,1)S(1)}) custom-call(bf16[256,1024]{1,0:T(8,128)(2,1)S(1)} %get-tuple-element.39.rows_hbm, f32[256,1024]{1,0:T(8,128)} %refs_7_.1, f32[1,256]{1,0:T(1,128)} %bitcast.7, s32[1,1536]{1,0:T(1,128)} %source_ref.15, s32[1,1536]{1,0:T(1,128)} %target_ref.15), custom_call_target="tpu_custom_call" | custom-call | flops 75497472 | bytes 589824 | tf_op jit(solution)/shard_map/pallas_call | solution.py:133
  22.1 0.0 copy-start
  22.2 2.1 %collective-permute-start.4 = (f32[584,128]{1,0:T(8,128)S(1)}, f32[584,128]{1,0:T(8,128)S(1)}, u32[]{:S(2)}, u32[]{:S(2)}) collective-permute-start(f32[584,128]{1,0:T(8,128)S(1)} %get-tuple-element.51), channel_id=1, source_target_pairs={{0,1},{1,2},{2,3},{3,4},{4,5},{5,6},{6,7},{7,8},{8,9},{9,10},{10,1... | collective-permute-start | bytes 897032 | tf_op jit(solution)/shard_map/ppermute | solution.py:255
  24.2 1.8 %shard_map.96 = (f32[584,128]{1,0:T(8,128)S(1)}, bf16[72,256]{1,0:T(8,128)(2,1)S(1)}) custom-call(bf16[256,1024]{1,0:T(8,128)(2,1)S(1)} %get-tuple-element.39.rows_hbm, f32[256,1024]{1,0:T(8,128)} %refs_7_.1, f32[1,256]{1,0:T(1,128)} %bitcast.8, s32[1,1536]{1,0:T(1,128)} %source_ref.15, s32[1,1536]{1,0:T(1,128)} %target_ref.15), custom_call_target="tpu_custom_call" | custom-call | flops 75497472 | bytes 589824 | tf_op jit(solution)/shard_map/pallas_call | solution.py:133
  26.0 1.9 %collective-permute-start.3 = (f32[584,128]{1,0:T(8,128)S(1)}, f32[584,128]{1,0:T(8,128)S(1)}, u32[]{:S(2)}, u32[]{:S(2)}) collective-permute-start(f32[584,128]{1,0:T(8,128)S(1)} %get-tuple-element.50), channel_id=1, source_target_pairs={{0,1},{1,2},{2,3},{3,4},{4,5},{5,6},{6,7},{7,8},{8,9},{9,10},{10,1... | collective-permute-start | bytes 897032 | tf_op jit(solution)/shard_map/ppermute | solution.py:255
  28.0 0.0 copy-start.4
  28.0 0.0 copy-done.1
  28.0 0.0 copy-done
  28.0 0.7 copy-done.4
  28.6 0.0 copy-start.2
  28.7 0.0 copy-start.3
  28.7 0.9 shard_map.97
  29.6 0.0 collective-permute-done.1.refs_1_
  29.6 2.5 %collective-permute-start.2 = (f32[456,128]{1,0:T(8,128)S(1)}, f32[456,128]{1,0:T(8,128)S(1)}, u32[]{:S(2)}, u32[]{:S(2)}) collective-permute-start(f32[456,128]{1,0:T(8,128)S(1)} %collective-permute-done.1.refs_1_), channel_id=1, source_target_pairs={{386,1},{387,2},{384,3},{385,4},{390,5},{391,6},{388,7},{389,8},{3... | collective-permute-start | bytes 700424 | tf_op jit(solution)/shard_map/ppermute | solution.py:253
  32.1 7.1 %collective-permute-done.block_ref.refs_4_ = f32[456,128]{1,0:T(8,128)S(1)} collective-permute-done((f32[456,128]{1,0:T(8,128)S(1)}, f32[456,128]{1,0:T(8,128)S(1)}, u32[]{:S(2)}, u32[]{:S(2)}) %collective-permute-start) | collective-permute-done | bytes 233504 | tf_op jit(solution)/shard_map/ppermute | solution.py:255
  39.2 0.0 copy-done.2
  39.2 0.0 copy-done.3
  39.2 0.8 shard_map.98
  39.9 1.9 %collective-permute-start.5 = (f32[456,128]{1,0:T(8,128)S(1)}, f32[456,128]{1,0:T(8,128)S(1)}, u32[]{:S(2)}, u32[]{:S(2)}) collective-permute-start(f32[456,128]{1,0:T(8,128)S(1)} %get-tuple-element.54), channel_id=1, source_target_pairs={{0,386},{1,387},{2,384},{3,385},{4,390},{5,391},{6,388},{7,389},{8... | collective-permute-start | bytes 700424 | tf_op jit(solution)/shard_map/ppermute | solution.py:252
  41.9 10.0 %collective-permute-done.4.block_ref.refs_6_ = f32[584,128]{1,0:T(8,128)S(1)} collective-permute-done((f32[584,128]{1,0:T(8,128)S(1)}, f32[584,128]{1,0:T(8,128)S(1)}, u32[]{:S(2)}, u32[]{:S(2)}) %collective-permute-start.4) | collective-permute-done | bytes 299040 | tf_op jit(solution)/shard_map/ppermute | solution.py:255
  51.8 0.8 shard_map.99
  52.6 1.9 %collective-permute-start.9 = (f32[584,128]{1,0:T(8,128)S(1)}, f32[584,128]{1,0:T(8,128)S(1)}, u32[]{:S(2)}, u32[]{:S(2)}) collective-permute-start(f32[584,128]{1,0:T(8,128)S(1)} %get-tuple-element.61), channel_id=1, source_target_pairs={{0,1},{1,2},{2,3},{3,4},{4,5},{5,6},{6,7},{7,8},{8,9},{9,10},{10,1... | collective-permute-start | bytes 897032 | tf_op jit(solution)/shard_map/ppermute | solution.py:255
  54.5 7.7 %collective-permute-done.3.block_ref.refs_7_ = f32[584,128]{1,0:T(8,128)S(1)} collective-permute-done((f32[584,128]{1,0:T(8,128)S(1)}, f32[584,128]{1,0:T(8,128)S(1)}, u32[]{:S(2)}, u32[]{:S(2)}) %collective-permute-start.3) | collective-permute-done | bytes 299040 | tf_op jit(solution)/shard_map/ppermute | solution.py:255
  62.2 0.8 shard_map.100
  63.0 1.9 %collective-permute-start.8 = (f32[584,128]{1,0:T(8,128)S(1)}, f32[584,128]{1,0:T(8,128)S(1)}, u32[]{:S(2)}, u32[]{:S(2)}) collective-permute-start(f32[584,128]{1,0:T(8,128)S(1)} %get-tuple-element.60), channel_id=1, source_target_pairs={{0,1},{1,2},{2,3},{3,4},{4,5},{5,6},{6,7},{7,8},{8,9},{9,10},{10,1... | collective-permute-start | bytes 897032 | tf_op jit(solution)/shard_map/ppermute | solution.py:255
  64.9 0.0 collective-permute-done.2.block_ref.refs_5_
  64.9 3.1 %collective-permute-done.5.refs_1_ = f32[456,128]{1,0:T(8,128)S(1)} collective-permute-done((f32[456,128]{1,0:T(8,128)S(1)}, f32[456,128]{1,0:T(8,128)S(1)}, u32[]{:S(2)}, u32[]{:S(2)}) %collective-permute-start.5) | collective-permute-done | bytes 233504 | tf_op jit(solution)/shard_map/ppermute | solution.py:252
  68.0 0.8 shard_map.101
  68.8 2.3 %collective-permute-start.7 = (f32[456,128]{1,0:T(8,128)S(1)}, f32[456,128]{1,0:T(8,128)S(1)}, u32[]{:S(2)}, u32[]{:S(2)}) collective-permute-start(f32[456,128]{1,0:T(8,128)S(1)} %get-tuple-element.59), channel_id=1, source_target_pairs={{0,1},{1,2},{2,3},{3,4},{4,5},{5,6},{6,7},{7,8},{8,9},{9,10},{10,1... | collective-permute-start | bytes 700424 | tf_op jit(solution)/shard_map/ppermute | solution.py:255
  71.0 1.9 %collective-permute-start.6 = (f32[456,128]{1,0:T(8,128)S(1)}, f32[456,128]{1,0:T(8,128)S(1)}, u32[]{:S(2)}, u32[]{:S(2)}) collective-permute-start(f32[456,128]{1,0:T(8,128)S(1)} %collective-permute-done.5.refs_1_), channel_id=1, source_target_pairs={{386,1},{387,2},{384,3},{385,4},{390,5},{391,6},{388,7},{389,8},{3... | collective-permute-start | bytes 700424 | tf_op jit(solution)/shard_map/ppermute | solution.py:253
  73.0 0.9 shard_map.102
  73.9 1.0 collective-permute-done.9.block_ref.refs_6_
  74.9 0.8 shard_map.103
  75.6 1.9 %collective-permute-start.12 = (f32[584,128]{1,0:T(8,128)S(1)}, f32[584,128]{1,0:T(8,128)S(1)}, u32[]{:S(2)}, u32[]{:S(2)}) collective-permute-start(f32[584,128]{1,0:T(8,128)S(1)} %get-tuple-element.70), channel_id=1, source_target_pairs={{0,48},{1,49},{2,50},{3,51},{4,52},{5,53},{6,54},{7,55},{8,56},{9,... | collective-permute-start | bytes 897032 | tf_op jit(solution)/shard_map/ppermute | solution.py:250
  77.6 12.7 %collective-permute-done.8.block_ref.refs_7_ = f32[584,128]{1,0:T(8,128)S(1)} collective-permute-done((f32[584,128]{1,0:T(8,128)S(1)}, f32[584,128]{1,0:T(8,128)S(1)}, u32[]{:S(2)}, u32[]{:S(2)}) %collective-permute-start.8) | collective-permute-done | bytes 299040 | tf_op jit(solution)/shard_map/ppermute | solution.py:255
  90.3 0.8 shard_map.104
  91.0 1.9 %collective-permute-start.13 = (f32[584,128]{1,0:T(8,128)S(1)}, f32[584,128]{1,0:T(8,128)S(1)}, u32[]{:S(2)}, u32[]{:S(2)}) collective-permute-start(f32[584,128]{1,0:T(8,128)S(1)} %get-tuple-element.71), channel_id=1, source_target_pairs={{0,48},{1,49},{2,50},{3,51},{4,52},{5,53},{6,54},{7,55},{8,56},{9,... | collective-permute-start | bytes 897032 | tf_op jit(solution)/shard_map/ppermute | solution.py:250
  93.0 4.6 %collective-permute-done.7.block_ref.refs_5_ = f32[456,128]{1,0:T(8,128)S(1)} collective-permute-done((f32[456,128]{1,0:T(8,128)S(1)}, f32[456,128]{1,0:T(8,128)S(1)}, u32[]{:S(2)}, u32[]{:S(2)}) %collective-permute-start.7) | collective-permute-done | bytes 233504 | tf_op jit(solution)/shard_map/ppermute | solution.py:255
  97.5 0.8 shard_map.105
  98.3 0.0 collective-permute-done.6.block_ref.refs_4_
  98.3 0.8 shard_map.106
  99.1 1.9 %collective-permute-start.10 = (f32[456,128]{1,0:T(8,128)S(1)}, f32[456,128]{1,0:T(8,128)S(1)}, u32[]{:S(2)}, u32[]{:S(2)}) collective-permute-start(f32[456,128]{1,0:T(8,128)S(1)} %get-tuple-element.68), channel_id=1, source_target_pairs={{0,48},{1,49},{2,50},{3,51},{4,52},{5,53},{6,54},{7,55},{8,56},{9,... | collective-permute-start | bytes 700424 | tf_op jit(solution)/shard_map/ppermute | solution.py:250
  101.0 3.5 %collective-permute-start.11 = (f32[456,128]{1,0:T(8,128)S(1)}, f32[456,128]{1,0:T(8,128)S(1)}, u32[]{:S(2)}, u32[]{:S(2)}) collective-permute-start(f32[456,128]{1,0:T(8,128)S(1)} %get-tuple-element.69), channel_id=1, source_target_pairs={{0,48},{1,49},{2,50},{3,51},{4,52},{5,53},{6,54},{7,55},{8,56},{9,... | collective-permute-start | bytes 700424 | tf_op jit(solution)/shard_map/ppermute | solution.py:250
  104.5 1.9 %shard_map.107 = (f32[256,1024]{1,0:T(8,128)}, f32[1,256]{1,0:T(1,128)}) custom-call(f32[256,1024]{1,0:T(8,128)S(1)} %get-tuple-element.56.rows_ref, f32[1,256]{1,0:T(1,128)S(1)} %get-tuple-element.57.state_ref, bf16[56,256]{1,0:T(8,128)(2,1)S(1)} %get-tuple-element.65.refs_0_, bf16[56,256]{1,0:T(8,128)(2,1)S(1)} %get-tuple-element.64.refs_0_.refs_1_, ...), custom_call_target="tpu_custom_call" | custom-call | flops 134217728 | bytes 3145728 | tf_op jit(solution)/shard_map/pallas_call | solution.py:196
  106.4 0.0 collective-permute-done.12.refs_2_
  106.4 0.0 collective-permute-done.13.refs_3_
  106.4 2.2 %collective-permute-done.10.refs_0_ = f32[456,128]{1,0:T(8,128)S(1)} collective-permute-done((f32[456,128]{1,0:T(8,128)S(1)}, f32[456,128]{1,0:T(8,128)S(1)}, u32[]{:S(2)}, u32[]{:S(2)}) %collective-permute-start.10) | collective-permute-done | bytes 233504 | tf_op jit(solution)/shard_map/ppermute | solution.py:250
  108.6 2.5 %collective-permute-done.11.refs_1_ = f32[456,128]{1,0:T(8,128)S(1)} collective-permute-done((f32[456,128]{1,0:T(8,128)S(1)}, f32[456,128]{1,0:T(8,128)S(1)}, u32[]{:S(2)}, u32[]{:S(2)}) %collective-permute-start.11) | collective-permute-done | bytes 233504 | tf_op jit(solution)/shard_map/ppermute | solution.py:250
  111.1 1.0 shard_map.108
Async XLA Ops:
  2.8 26.8 %collective-permute-start.1 = (f32[456,128]{1,0:T(8,128)S(1)}, f32[456,128]{1,0:T(8,128)S(1)}, u32[]{:S(2)}, u32[]{:S(2)}) collective-permute-start(f32[456,128]{1,0:T(8,128)S(1)} %get-tuple-element.49), channel_id=1, source_target_pairs={{0,386},{1,387},{2,384},{3,385},{4,390},{5,391},{6,388},{7,389},{8... | collective-permute-start | bytes 700424 | tf_op jit(solution)/shard_map/ppermute | solution.py:252
  10.6 28.5 %collective-permute-start = (f32[456,128]{1,0:T(8,128)S(1)}, f32[456,128]{1,0:T(8,128)S(1)}, u32[]{:S(2)}, u32[]{:S(2)}) collective-permute-start(f32[456,128]{1,0:T(8,128)S(1)} %get-tuple-element.47), channel_id=1, source_target_pairs={{0,1},{1,2},{2,3},{3,4},{4,5},{5,6},{6,7},{7,8},{8,9},{9,10},{10,1... | collective-permute-start | bytes 700424 | tf_op jit(solution)/shard_map/ppermute | solution.py:255
  20.2 7.8 %copy-start.1 = (f32[256,1024]{1,0:T(8,128)S(1)}, f32[256,1024]{1,0:T(8,128)}, u32[]{:S(2)}) copy-start(f32[256,1024]{1,0:T(8,128)} %rows_ref.1) | copy-start | bytes 3145732
  22.1 5.8 %copy-start = (f32[256,1024]{1,0:T(8,128)S(1)}, f32[256,1024]{1,0:T(8,128)}, u32[]{:S(2)}) copy-start(f32[256,1024]{1,0:T(8,128)} %refs_7_.1) | copy-start | bytes 3145732
  22.2 29.7 %collective-permute-start.4 = (f32[584,128]{1,0:T(8,128)S(1)}, f32[584,128]{1,0:T(8,128)S(1)}, u32[]{:S(2)}, u32[]{:S(2)}) collective-permute-start(f32[584,128]{1,0:T(8,128)S(1)} %get-tuple-element.51), channel_id=1, source_target_pairs={{0,1},{1,2},{2,3},{3,4},{4,5},{5,6},{6,7},{7,8},{8,9},{9,10},{10,1... | collective-permute-start | bytes 897032 | tf_op jit(solution)/shard_map/ppermute | solution.py:255
  26.0 36.2 %collective-permute-start.3 = (f32[584,128]{1,0:T(8,128)S(1)}, f32[584,128]{1,0:T(8,128)S(1)}, u32[]{:S(2)}, u32[]{:S(2)}) collective-permute-start(f32[584,128]{1,0:T(8,128)S(1)} %get-tuple-element.50), channel_id=1, source_target_pairs={{0,1},{1,2},{2,3},{3,4},{4,5},{5,6},{6,7},{7,8},{8,9},{9,10},{10,1... | collective-permute-start | bytes 897032 | tf_op jit(solution)/shard_map/ppermute | solution.py:255
  28.0 0.7 copy-start.4
  28.6 10.5 %copy-start.2 = (s32[1,1536]{1,0:T(1,128)S(1)}, s32[1,1536]{1,0:T(1,128)}, u32[]{:S(2)}) copy-start(s32[1,1536]{1,0:T(1,128)} %source_ref.15) | copy-start | bytes 18436
  28.7 10.5 %copy-start.3 = (s32[1,1536]{1,0:T(1,128)S(1)}, s32[1,1536]{1,0:T(1,128)}, u32[]{:S(2)}) copy-start(s32[1,1536]{1,0:T(1,128)} %target_ref.15) | copy-start | bytes 18436
  29.6 35.3 %collective-permute-start.2 = (f32[456,128]{1,0:T(8,128)S(1)}, f32[456,128]{1,0:T(8,128)S(1)}, u32[]{:S(2)}, u32[]{:S(2)}) collective-permute-start(f32[456,128]{1,0:T(8,128)S(1)} %collective-permute-done.1.refs_1_), channel_id=1, source_target_pairs={{386,1},{387,2},{384,3},{385,4},{390,5},{391,6},{388,7},{389,8},{3... | collective-permute-start | bytes 700424 | tf_op jit(solution)/shard_map/ppermute | solution.py:253
  39.9 28.1 %collective-permute-start.5 = (f32[456,128]{1,0:T(8,128)S(1)}, f32[456,128]{1,0:T(8,128)S(1)}, u32[]{:S(2)}, u32[]{:S(2)}) collective-permute-start(f32[456,128]{1,0:T(8,128)S(1)} %get-tuple-element.54), channel_id=1, source_target_pairs={{0,386},{1,387},{2,384},{3,385},{4,390},{5,391},{6,388},{7,389},{8... | collective-permute-start | bytes 700424 | tf_op jit(solution)/shard_map/ppermute | solution.py:252
  52.6 22.3 %collective-permute-start.9 = (f32[584,128]{1,0:T(8,128)S(1)}, f32[584,128]{1,0:T(8,128)S(1)}, u32[]{:S(2)}, u32[]{:S(2)}) collective-permute-start(f32[584,128]{1,0:T(8,128)S(1)} %get-tuple-element.61), channel_id=1, source_target_pairs={{0,1},{1,2},{2,3},{3,4},{4,5},{5,6},{6,7},{7,8},{8,9},{9,10},{10,1... | collective-permute-start | bytes 897032 | tf_op jit(solution)/shard_map/ppermute | solution.py:255
  63.0 27.3 %collective-permute-start.8 = (f32[584,128]{1,0:T(8,128)S(1)}, f32[584,128]{1,0:T(8,128)S(1)}, u32[]{:S(2)}, u32[]{:S(2)}) collective-permute-start(f32[584,128]{1,0:T(8,128)S(1)} %get-tuple-element.60), channel_id=1, source_target_pairs={{0,1},{1,2},{2,3},{3,4},{4,5},{5,6},{6,7},{7,8},{8,9},{9,10},{10,1... | collective-permute-start | bytes 897032 | tf_op jit(solution)/shard_map/ppermute | solution.py:255
  68.8 28.8 %collective-permute-start.7 = (f32[456,128]{1,0:T(8,128)S(1)}, f32[456,128]{1,0:T(8,128)S(1)}, u32[]{:S(2)}, u32[]{:S(2)}) collective-permute-start(f32[456,128]{1,0:T(8,128)S(1)} %get-tuple-element.59), channel_id=1, source_target_pairs={{0,1},{1,2},{2,3},{3,4},{4,5},{5,6},{6,7},{7,8},{8,9},{9,10},{10,1... | collective-permute-start | bytes 700424 | tf_op jit(solution)/shard_map/ppermute | solution.py:255
  71.0 27.3 %collective-permute-start.6 = (f32[456,128]{1,0:T(8,128)S(1)}, f32[456,128]{1,0:T(8,128)S(1)}, u32[]{:S(2)}, u32[]{:S(2)}) collective-permute-start(f32[456,128]{1,0:T(8,128)S(1)} %collective-permute-done.5.refs_1_), channel_id=1, source_target_pairs={{386,1},{387,2},{384,3},{385,4},{390,5},{391,6},{388,7},{389,8},{3... | collective-permute-start | bytes 700424 | tf_op jit(solution)/shard_map/ppermute | solution.py:253
  75.6 30.7 %collective-permute-start.12 = (f32[584,128]{1,0:T(8,128)S(1)}, f32[584,128]{1,0:T(8,128)S(1)}, u32[]{:S(2)}, u32[]{:S(2)}) collective-permute-start(f32[584,128]{1,0:T(8,128)S(1)} %get-tuple-element.70), channel_id=1, source_target_pairs={{0,48},{1,49},{2,50},{3,51},{4,52},{5,53},{6,54},{7,55},{8,56},{9,... | collective-permute-start | bytes 897032 | tf_op jit(solution)/shard_map/ppermute | solution.py:250
  91.0 15.3 %collective-permute-start.13 = (f32[584,128]{1,0:T(8,128)S(1)}, f32[584,128]{1,0:T(8,128)S(1)}, u32[]{:S(2)}, u32[]{:S(2)}) collective-permute-start(f32[584,128]{1,0:T(8,128)S(1)} %get-tuple-element.71), channel_id=1, source_target_pairs={{0,48},{1,49},{2,50},{3,51},{4,52},{5,53},{6,54},{7,55},{8,56},{9,... | collective-permute-start | bytes 897032 | tf_op jit(solution)/shard_map/ppermute | solution.py:250
  99.1 9.5 %collective-permute-start.10 = (f32[456,128]{1,0:T(8,128)S(1)}, f32[456,128]{1,0:T(8,128)S(1)}, u32[]{:S(2)}, u32[]{:S(2)}) collective-permute-start(f32[456,128]{1,0:T(8,128)S(1)} %get-tuple-element.68), channel_id=1, source_target_pairs={{0,48},{1,49},{2,50},{3,51},{4,52},{5,53},{6,54},{7,55},{8,56},{9,... | collective-permute-start | bytes 700424 | tf_op jit(solution)/shard_map/ppermute | solution.py:250
  101.0 10.1 %collective-permute-start.11 = (f32[456,128]{1,0:T(8,128)S(1)}, f32[456,128]{1,0:T(8,128)S(1)}, u32[]{:S(2)}, u32[]{:S(2)}) collective-permute-start(f32[456,128]{1,0:T(8,128)S(1)} %get-tuple-element.69), channel_id=1, source_target_pairs={{0,48},{1,49},{2,50},{3,51},{4,52},{5,53},{6,54},{7,55},{8,56},{9,... | collective-permute-start | bytes 700424 | tf_op jit(solution)/shard_map/ppermute | solution.py:250

commit v4 on v3

--- a/solution.py
+++ b/solution.py
@@ -13,7 +13,7 @@
 LANES = 128
 STATES = 8
 CHUNKS = ((0, 56, False, True), (56, 56, True, False), (112, 72, False, False), (184, 72, False, False))
-ORDERS = ((1, 0, 2, 3), (0, 2, 3, 1), (2, 3, 1, 0))
+ORDERS = ((0, 1, 2, 3), (0, 2, 3, 1), (2, 3, 0, 1))
 RELAYS = {(1, 2): ((0, 1),), (1, 1): ((1, 0),)}
 LIMIT = 40 << 20
 HBM = pl.BlockSpec(memory_space=pltpu.HBM)
@@ -36,6 +36,16 @@
             y = (i % Y_HI * Y_LO + o // share - 3) % (Y_HI * Y_LO)
             pairs.append((o * n_inner + i, (y % Y_LO * share + o % share) * n_inner + i - i % Y_HI + y // Y_LO))
     return pairs
+
+
+def mirror(n_outer, n_inner):
+    n_z = n_inner // Y_HI
+    return [
+        (o * n_inner + z * Y_HI + y, o * n_inner + (n_z - 1 - z) * Y_HI + y)
+        for o in range(n_outer)
+        for z in range((n_z + 1) // 2, n_z)
+        for y in range(Y_HI)
+    ]
 
 
 def dot(a, b, contract):
@@ -87,29 +97,43 @@
 
 
 def first_kernel(first, size, rows_hbm, block_hbm, state_hbm, source_hbm, target_hbm, *refs):
-    outs, scratch = refs[:-6], refs[-6:]
-    new_ref, grad_ref = outs[0], outs[1]
-    rows_ref, block_ref, state_ref, source_ref, target_ref, sems = scratch
+    new_ref, grad_ref, rounded_ref, block_ref, state_ref, source_ref, target_ref, rows_ref, sems = refs
+    mine = pl.ds(first, size)
     pairs = [
         (source_hbm, source_ref),
         (target_hbm, target_ref),
         (state_hbm, state_ref),
         (rows_hbm, rows_ref),
-        (block_hbm.at[pl.ds(first, size), :], block_ref),
+        (block_hbm.at[mine, :], block_ref.at[mine, :]),
     ]
+    count = rows_ref.shape[0]
+    if first > 0:
+        pairs.append((block_hbm.at[pl.ds(0, first), :], block_ref.at[pl.ds(0, first), :]))
+    if first + size < count:
+        rest = pl.ds(first + size, count - first - size)
+        pairs.append((block_hbm.at[rest, :], block_ref.at[rest, :]))
     copies = [pltpu.make_async_copy(a, b, sems.at[k]) for k, (a, b) in enumerate(pairs)]
     for copy in copies:
         copy.start()
     for copy in copies[:3]:
         copy.wait()
-    edges = source_ref.shape[1] // ROUNDS
-    counts = edge_counts(source_ref, target_ref, 0, edges, first, size, rows_ref.shape[0])
+    counts = edge_counts(source_ref, target_ref, 0, source_ref.shape[1] // ROUNDS, first, size, count)
     copies[3].wait()
     rows_b = rows_ref[...].astype(jnp.bfloat16)
-    if len(outs) > 2:
-        outs[2][...] = rows_b
+    rounded_ref[...] = rows_b
     copies[4].wait()
-    update_chunk(first, rows_b, block_ref[...], state_ref[...], counts, new_ref, grad_ref)
+    update_chunk(first, rows_b, block_ref[mine, :], state_ref[...], counts, new_ref, grad_ref)
+    for copy in copies[5:]:
+        copy.wait()
+
+
+def rest_kernel(chunks, rows_ref, block_ref, state_ref, source_ref, target_ref, *refs):
+    outs = refs[-2 * len(chunks) :]
+    edges = source_ref.shape[1] // ROUNDS
+    for (first, size, *_), new_ref, grad_ref in zip(chunks, outs[::2], outs[1::2], strict=True):
+        counts = edge_counts(source_ref, target_ref, 0, edges, first, size, rows_ref.shape[0])
+        block = block_ref[pl.ds(first, size), :]
+        update_chunk(first, rows_ref[...], block, state_ref[...], counts, new_ref, grad_ref)
 
 
 def chunk_outs(size, count, width):
@@ -127,25 +151,30 @@
 
 def meet_first(rows, context, state, source, target, first, size):
     count, width = rows.shape
-    out = chunk_outs(size, count, width)
-    if rows.dtype == jnp.float32:
-        out.append(jax.ShapeDtypeStruct(rows.shape, jnp.bfloat16))
+    out = chunk_outs(size, count, width) + [jax.ShapeDtypeStruct(rows.shape, jnp.bfloat16)]
+    out += [jax.ShapeDtypeStruct(array.shape, array.dtype) for array in (context, state, source, target)]
     return pl.pallas_call(
         functools.partial(first_kernel, first, size),
         out_shape=out,
-        in_specs=[HBM if rows.dtype == jnp.float32 else pl.BlockSpec(memory_space=pl.ANY)] + [HBM] * 4,
+        in_specs=[HBM] * 5,
         out_specs=[VMEM] * len(out),
-        scratch_shapes=[
-            pltpu.VMEM(rows.shape, rows.dtype),
-            pltpu.VMEM((size, width), jnp.float32),
-            pltpu.VMEM(state.shape, jnp.float32),
-            pltpu.VMEM(source.shape, jnp.int32),
-            pltpu.VMEM(target.shape, jnp.int32),
-            pltpu.SemaphoreType.DMA((5,)),
-        ],
+        scratch_shapes=[pltpu.VMEM(rows.shape, rows.dtype), pltpu.SemaphoreType.DMA((7,))],
         cost_estimate=chunk_cost(size, count, width),
         compiler_params=pltpu.CompilerParams(vmem_limit_bytes=LIMIT),
     )(rows, context, state, source, target)
+
+
+def meet_rest(chunks, rows_b, kept, after):
+    count, width = rows_b.shape
+    out = [shape for _, size, *_ in chunks for shape in chunk_outs(size, count, width)]
+    return pl.pallas_call(
+        functools.partial(rest_kernel, chunks),
+        out_shape=out,
+        in_specs=[VMEM] * 5 + [pl.BlockSpec(memory_space=pl.ANY)] * len(after),
+        out_specs=[VMEM] * len(out),
+        cost_estimate=chunk_cost(sum(size for _, size, *_ in chunks), count, width),
+        compiler_params=pltpu.CompilerParams(vmem_limit_bytes=LIMIT),
+    )(rows_b, *kept, *after)
 
 
 def meet_kernel(first, step, edges, rows_ref, block_ref, source_ref, target_ref, *refs):
@@ -231,20 +260,26 @@
     direct, relays = step_inner(*places), dict(halfway(*places))
     whole = [vertex, context, context_state.reshape(1, -1), edge_source, edge_target]
     whole = [pltpu.with_memory_space_constraint(array, pltpu.HBM) for array in whole]
-    rows, row_state, rows_b = vertex, vertex_state.reshape(1, -1), whole[0]
-    blocks = [context] * len(CHUNKS)
+    rows, row_state = vertex, vertex_state.reshape(1, -1)
+    signal = lax.ppermute(vertex_state, BOTH, mirror(*places))
     legs = {}
     for step in range(ROUNDS):
         last = step == ROUNDS - 1
         moved, grads, previous = {}, {}, []
+        if step == 0:
+            front, *others = ORDERS[0]
+            new, grad, rows_b, *kept = meet_first(*whole, *CHUNKS[front][:2])
+            new, grad, signal = lax.optimization_barrier((new, grad, signal))
+            pairs = meet_rest([CHUNKS[k] for k in others], rows_b, kept, [grad, signal])
+            met = {front: (new, grad)} | {k: tuple(pairs[2 * j : 2 * j + 2]) for j, k in enumerate(others)}
+            blocks, source, target = [kept[0]] * len(CHUNKS), *kept[2:]
         for k in ORDERS[step]:
             first, size, *long_way = CHUNKS[k]
             after = previous + [legs[at] for at in RELAYS.get((step, k), ())]
             if step == 0:
-                new, grad, *more = meet_first(rows_b, *whole[1:], first, size)
-                rows_b = more[0] if more else rows_b
+                new, grad = met[k]
             else:
-                new, grad = meet(rows_b, blocks[k], edge_source, edge_target, after, first, size, step)
+                new, grad = meet(rows_b, blocks[k], source, target, after, first, size, step)
             previous, grads[k] = [grad], grad
             if last:
                 moved[k] = lax.ppermute(new, BOTH, step_outer(*places))

time: 113 us -> 111 us (0.982)
  the two profiles are of different devices: /device:TPU:8 before, /device:TPU:16 now
where the time goes in v4:
time: 111 us
  starting transfers between devices  65.7 us (59%)
  waiting for transfers between devices  28.7 us (26%)
  Pallas kernels  14.6 us (13%)
    ppermute x6, starting transfers between devices, body(): moved[k] = lax.ppermute(new, BOTH, direct)  34.7 us
    ppermute x2, starting transfers between devices, body(): lax.ppermute(legs[step, k], BOTH, [(relays[p], q) for p, q in direct])  12.9 us
    ppermute x1, waiting for transfers between devices, body(): signal = lax.ppermute(vertex_state, BOTH, mirror(*places))  12.2 us
    ppermute x4, starting transfers between devices, body(): moved[k] = lax.ppermute(new, BOTH, step_outer(*places))  10.9 us
    ppermute x2, waiting for transfers between devices, body(): lax.ppermute(legs[step, k], BOTH, [(relays[p], q) for p, q in direct])  6.38 us
    pallas_call x8, Pallas kernels, meet(): pl.pallas_call(functools.partial(meet_kernel, first, step, source.shape[1...  6.11 us
    ppermute x2, starting transfers between devices, body(): legs[step, k] = lax.ppermute(new, BOTH, list(relays.items()))  5.83 us
    ppermute x6, waiting for transfers between devices, body(): moved[k] = lax.ppermute(new, BOTH, direct)  5.24 us
  transfers between devices with their start and end apart: 15, of which 6 were waited for; matrix products, arithmetic and copies ran while one was open for 0% of the time, Pallas kernels for 12%

profile of v4, /device:TPU:16, one launch (start us, length us, event | category | flops | bytes accessed | tf_op | source)
XLA Modules:
  0.0 110.6 jit_solution(13722688374011556777)
XLA Ops:
  0.6 1.3 %collective-permute-start = (f32[256]{0:T(256)}, f32[256]{0:T(256)S(1)}, u32[]{:S(2)}, u32[]{:S(2)}) collective-permute-start(f32[256]{0:T(256)} %param.7), channel_id=1, source_target_pairs={{24,20},{25,21},{26,22},{27,23},{28,16},{29,17},{30,18},{31,19},{3... | collective-permute-start | bytes 3080 | tf_op jit(solution)/shard_map/ppermute | solution.py:264
  1.9 2.1 %shard_map.93 = (f32[456,128]{1,0:T(8,128)S(1)}, bf16[56,256]{1,0:T(8,128)(2,1)S(1)}, bf16[256,1024]{1,0:T(8,128)(2,1)S(1)}, f32[256,1024]{1,0:T(8,128)S(1)}, f3...) custom-call(f32[256,1024]{1,0:T(8,128)} %rows_ref.1, f32[256,1024]{1,0:T(8,128)} %block_hbm.1, ...), custom_call_target="tpu_custom_call" | custom-call | flops 58720256 | bytes 458752 | tf_op jit(solution)/shard_map/pallas_call | solution.py:156
  4.1 0.0 copy-start
  4.1 12.2 %collective-permute-done.refs_1_ = f32[256]{0:T(256)S(1)} collective-permute-done((f32[256]{0:T(256)}, f32[256]{0:T(256)S(1)}, u32[]{:S(2)}, u32[]{:S(2)}) %collective-permute-start) | collective-permute-done | bytes 1056 | tf_op jit(solution)/shard_map/ppermute | solution.py:264
  16.3 5.7 %collective-permute-start.1 = (f32[456,128]{1,0:T(8,128)S(1)}, f32[456,128]{1,0:T(8,128)S(1)}, u32[]{:S(2)}, u32[]{:S(2)}) collective-permute-start(f32[456,128]{1,0:T(8,128)S(1)} %get-tuple-element.61), channel_id=1, source_target_pairs={{0,1},{1,2},{2,3},{3,4},{4,5},{5,6},{6,7},{7,8},{8,9},{9,10},{10,1... | collective-permute-start | bytes 700424 | tf_op jit(solution)/shard_map/ppermute | solution.py:290
  22.1 1.6 %shard_map.94 = (f32[456,128]{1,0:T(8,128)S(1)}, bf16[56,256]{1,0:T(8,128)(2,1)S(1)}, f32[584,128]{1,0:T(8,128)S(1)}, bf16[72,256]{1,0:T(8,128)(2,1)S(1)}, f32[5...) custom-call(bf16[256,1024]{1,0:T(8,128)(2,1)S(1)} %get-tuple-element.49.rows_ref, ...), custom_call_target="tpu_custom_call" | custom-call | flops 209715200 | bytes 1638400 | tf_op jit(solution)/shard_map/pallas_call | solution.py:170
  23.6 3.0 %collective-permute-start.2 = (f32[456,128]{1,0:T(8,128)S(1)}, f32[456,128]{1,0:T(8,128)S(1)}, u32[]{:S(2)}, u32[]{:S(2)}) collective-permute-start(f32[456,128]{1,0:T(8,128)S(1)} %get-tuple-element.63), channel_id=1, source_target_pairs={{0,386},{1,387},{2,384},{3,385},{4,390},{5,391},{6,388},{7,389},{8... | collective-permute-start | bytes 700424 | tf_op jit(solution)/shard_map/ppermute | solution.py:287
  26.6 3.6 %collective-permute-start.5 = (f32[584,128]{1,0:T(8,128)S(1)}, f32[584,128]{1,0:T(8,128)S(1)}, u32[]{:S(2)}, u32[]{:S(2)}) collective-permute-start(f32[584,128]{1,0:T(8,128)S(1)} %get-tuple-element.65), channel_id=1, source_target_pairs={{0,1},{1,2},{2,3},{3,4},{4,5},{5,6},{6,7},{7,8},{8,9},{9,10},{10,1... | collective-permute-start | bytes 897032 | tf_op jit(solution)/shard_map/ppermute | solution.py:290
  30.3 4.8 %collective-permute-start.4 = (f32[584,128]{1,0:T(8,128)S(1)}, f32[584,128]{1,0:T(8,128)S(1)}, u32[]{:S(2)}, u32[]{:S(2)}) collective-permute-start(f32[584,128]{1,0:T(8,128)S(1)} %get-tuple-element.64), channel_id=1, source_target_pairs={{0,1},{1,2},{2,3},{3,4},{4,5},{5,6},{6,7},{7,8},{8,9},{9,10},{10,1... | collective-permute-start | bytes 897032 | tf_op jit(solution)/shard_map/ppermute | solution.py:290
  35.1 0.0 copy-start.1
  35.1 0.0 copy-done
  35.1 0.7 copy-done.1
  35.8 0.9 shard_map.95
  36.7 0.0 collective-permute-done.1.block_ref.refs_4_
  36.7 0.8 shard_map.96
  37.5 2.8 %collective-permute-start.6 = (f32[456,128]{1,0:T(8,128)S(1)}, f32[456,128]{1,0:T(8,128)S(1)}, u32[]{:S(2)}, u32[]{:S(2)}) collective-permute-start(f32[456,128]{1,0:T(8,128)S(1)} %get-tuple-element.68), channel_id=1, source_target_pairs={{0,386},{1,387},{2,384},{3,385},{4,390},{5,391},{6,388},{7,389},{8... | collective-permute-start | bytes 700424 | tf_op jit(solution)/shard_map/ppermute | solution.py:287
  40.3 0.2 collective-permute-done.2.refs_1_
  40.5 9.7 %collective-permute-start.3 = (f32[456,128]{1,0:T(8,128)S(1)}, f32[456,128]{1,0:T(8,128)S(1)}, u32[]{:S(2)}, u32[]{:S(2)}) collective-permute-start(f32[456,128]{1,0:T(8,128)S(1)} %collective-permute-done.2.refs_1_), channel_id=1, source_target_pairs={{386,1},{387,2},{384,3},{385,4},{390,5},{391,6},{388,7},{389,8},{3... | collective-permute-start | bytes 700424 | tf_op jit(solution)/shard_map/ppermute | solution.py:288
  50.2 0.0 collective-permute-done.5.block_ref.refs_6_
  50.2 0.8 shard_map.97
  51.0 4.9 %collective-permute-start.9 = (f32[584,128]{1,0:T(8,128)S(1)}, f32[584,128]{1,0:T(8,128)S(1)}, u32[]{:S(2)}, u32[]{:S(2)}) collective-permute-start(f32[584,128]{1,0:T(8,128)S(1)} %get-tuple-element.74), channel_id=1, source_target_pairs={{0,1},{1,2},{2,3},{3,4},{4,5},{5,6},{6,7},{7,8},{8,9},{9,10},{10,1... | collective-permute-start | bytes 897032 | tf_op jit(solution)/shard_map/ppermute | solution.py:290
  55.9 5.2 %collective-permute-done.4.block_ref.refs_7_ = f32[584,128]{1,0:T(8,128)S(1)} collective-permute-done((f32[584,128]{1,0:T(8,128)S(1)}, f32[584,128]{1,0:T(8,128)S(1)}, u32[]{:S(2)}, u32[]{:S(2)}) %collective-permute-start.4) | collective-permute-done | bytes 299040 | tf_op jit(solution)/shard_map/ppermute | solution.py:290
  61.1 0.8 shard_map.98
  61.9 6.9 %collective-permute-start.8 = (f32[584,128]{1,0:T(8,128)S(1)}, f32[584,128]{1,0:T(8,128)S(1)}, u32[]{:S(2)}, u32[]{:S(2)}) collective-permute-start(f32[584,128]{1,0:T(8,128)S(1)} %get-tuple-element.73), channel_id=1, source_target_pairs={{0,1},{1,2},{2,3},{3,4},{4,5},{5,6},{6,7},{7,8},{8,9},{9,10},{10,1... | collective-permute-start | bytes 897032 | tf_op jit(solution)/shard_map/ppermute | solution.py:290
  68.8 0.0 collective-permute-done.6.refs_1_
  68.8 3.3 %collective-permute-start.7 = (f32[456,128]{1,0:T(8,128)S(1)}, f32[456,128]{1,0:T(8,128)S(1)}, u32[]{:S(2)}, u32[]{:S(2)}) collective-permute-start(f32[456,128]{1,0:T(8,128)S(1)} %collective-permute-done.6.refs_1_), channel_id=1, source_target_pairs={{386,1},{387,2},{384,3},{385,4},{390,5},{391,6},{388,7},{389,8},{3... | collective-permute-start | bytes 700424 | tf_op jit(solution)/shard_map/ppermute | solution.py:288
  72.1 6.4 %collective-permute-done.3.block_ref.refs_5_ = f32[456,128]{1,0:T(8,128)S(1)} collective-permute-done((f32[456,128]{1,0:T(8,128)S(1)}, f32[456,128]{1,0:T(8,128)S(1)}, u32[]{:S(2)}, u32[]{:S(2)}) %collective-permute-start.3) | collective-permute-done | bytes 233504 | tf_op jit(solution)/shard_map/ppermute | solution.py:288
  78.5 0.8 shard_map.99
  79.3 8.7 %collective-permute-start.10 = (f32[456,128]{1,0:T(8,128)S(1)}, f32[456,128]{1,0:T(8,128)S(1)}, u32[]{:S(2)}, u32[]{:S(2)}) collective-permute-start(f32[456,128]{1,0:T(8,128)S(1)} %get-tuple-element.78), channel_id=1, source_target_pairs={{0,1},{1,2},{2,3},{3,4},{4,5},{5,6},{6,7},{7,8},{8,9},{9,10},{10,1... | collective-permute-start | bytes 700424 | tf_op jit(solution)/shard_map/ppermute | solution.py:290
  88.0 0.9 shard_map.100
  88.9 0.0 collective-permute-done.9.block_ref.refs_6_
  88.9 0.8 shard_map.101
  89.7 1.9 %collective-permute-start.13 = (f32[584,128]{1,0:T(8,128)S(1)}, f32[584,128]{1,0:T(8,128)S(1)}, u32[]{:S(2)}, u32[]{:S(2)}) collective-permute-start(f32[584,128]{1,0:T(8,128)S(1)} %get-tuple-element.84), channel_id=1, source_target_pairs={{0,48},{1,49},{2,50},{3,51},{4,52},{5,53},{6,54},{7,55},{8,56},{9,... | collective-permute-start | bytes 897032 | tf_op jit(solution)/shard_map/ppermute | solution.py:285
  91.6 0.0 collective-permute-done.8.block_ref.refs_7_
  91.6 0.8 shard_map.102
  92.4 3.6 %collective-permute-start.14 = (f32[584,128]{1,0:T(8,128)S(1)}, f32[584,128]{1,0:T(8,128)S(1)}, u32[]{:S(2)}, u32[]{:S(2)}) collective-permute-start(f32[584,128]{1,0:T(8,128)S(1)} %get-tuple-element.85), channel_id=1, source_target_pairs={{0,48},{1,49},{2,50},{3,51},{4,52},{5,53},{6,54},{7,55},{8,56},{9,... | collective-permute-start | bytes 897032 | tf_op jit(solution)/shard_map/ppermute | solution.py:285
  96.0 0.0 collective-permute-done.7.block_ref.refs_4_
  96.0 0.8 shard_map.103
  96.8 0.0 collective-permute-done.10.block_ref.refs_5_
  96.8 0.8 shard_map.104
  97.6 1.9 %collective-permute-start.12 = (f32[456,128]{1,0:T(8,128)S(1)}, f32[456,128]{1,0:T(8,128)S(1)}, u32[]{:S(2)}, u32[]{:S(2)}) collective-permute-start(f32[456,128]{1,0:T(8,128)S(1)} %get-tuple-element.83), channel_id=1, source_target_pairs={{0,48},{1,49},{2,50},{3,51},{4,52},{5,53},{6,54},{7,55},{8,56},{9,... | collective-permute-start | bytes 700424 | tf_op jit(solution)/shard_map/ppermute | solution.py:285
  99.5 3.5 %collective-permute-start.11 = (f32[456,128]{1,0:T(8,128)S(1)}, f32[456,128]{1,0:T(8,128)S(1)}, u32[]{:S(2)}, u32[]{:S(2)}) collective-permute-start(f32[456,128]{1,0:T(8,128)S(1)} %get-tuple-element.82), channel_id=1, source_target_pairs={{0,48},{1,49},{2,50},{3,51},{4,52},{5,53},{6,54},{7,55},{8,56},{9,... | collective-permute-start | bytes 700424 | tf_op jit(solution)/shard_map/ppermute | solution.py:285
  103.0 1.9 %shard_map.105 = (f32[256,1024]{1,0:T(8,128)}, f32[1,256]{1,0:T(1,128)}) custom-call(f32[256,1024]{1,0:T(8,128)S(1)} %get-tuple-element.70.rows_ref, f32[1,256]{1,0:T(1,128)S(1)} %get-tuple-element.71.state_ref, bf16[56,256]{1,0:T(8,128)(2,1)S(1)} %get-tuple-element.77.refs_0_, bf16[56,256]{1,0:T(8,128)(2,1)S(1)} %get-tuple-element.79.refs_1_, ...), custom_call_target="tpu_custom_call" | custom-call | flops 134217728 | bytes 3145728 | tf_op jit(solution)/shard_map/pallas_call | solution.py:225
  104.9 0.0 collective-permute-done.13.refs_2_
  104.9 0.0 collective-permute-done.14.refs_3_
  104.9 2.1 %collective-permute-done.12.refs_1_ = f32[456,128]{1,0:T(8,128)S(1)} collective-permute-done((f32[456,128]{1,0:T(8,128)S(1)}, f32[456,128]{1,0:T(8,128)S(1)}, u32[]{:S(2)}, u32[]{:S(2)}) %collective-permute-start.12) | collective-permute-done | bytes 233504 | tf_op jit(solution)/shard_map/ppermute | solution.py:285
  107.1 2.5 %collective-permute-done.11.refs_0_ = f32[456,128]{1,0:T(8,128)S(1)} collective-permute-done((f32[456,128]{1,0:T(8,128)S(1)}, f32[456,128]{1,0:T(8,128)S(1)}, u32[]{:S(2)}, u32[]{:S(2)}) %collective-permute-start.11) | collective-permute-done | bytes 233504 | tf_op jit(solution)/shard_map/ppermute | solution.py:285
  109.6 1.0 shard_map.106
Async XLA Ops:
  0.6 15.7 %collective-permute-start = (f32[256]{0:T(256)}, f32[256]{0:T(256)S(1)}, u32[]{:S(2)}, u32[]{:S(2)}) collective-permute-start(f32[256]{0:T(256)} %param.7), channel_id=1, source_target_pairs={{24,20},{25,21},{26,22},{27,23},{28,16},{29,17},{30,18},{31,19},{3... | collective-permute-start | bytes 3080 | tf_op jit(solution)/shard_map/ppermute | solution.py:264
  4.1 31.0 %copy-start = (f32[256,1024]{1,0:T(8,128)S(1)}, f32[256,1024]{1,0:T(8,128)}, u32[]{:S(2)}) copy-start(f32[256,1024]{1,0:T(8,128)} %rows_ref.1) | copy-start | bytes 3145732
  16.3 20.3 %collective-permute-start.1 = (f32[456,128]{1,0:T(8,128)S(1)}, f32[456,128]{1,0:T(8,128)S(1)}, u32[]{:S(2)}, u32[]{:S(2)}) collective-permute-start(f32[456,128]{1,0:T(8,128)S(1)} %get-tuple-element.61), channel_id=1, source_target_pairs={{0,1},{1,2},{2,3},{3,4},{4,5},{5,6},{6,7},{7,8},{8,9},{9,10},{10,1... | collective-permute-start | bytes 700424 | tf_op jit(solution)/shard_map/ppermute | solution.py:290
  23.6 16.9 %collective-permute-start.2 = (f32[456,128]{1,0:T(8,128)S(1)}, f32[456,128]{1,0:T(8,128)S(1)}, u32[]{:S(2)}, u32[]{:S(2)}) collective-permute-start(f32[456,128]{1,0:T(8,128)S(1)} %get-tuple-element.63), channel_id=1, source_target_pairs={{0,386},{1,387},{2,384},{3,385},{4,390},{5,391},{6,388},{7,389},{8... | collective-permute-start | bytes 700424 | tf_op jit(solution)/shard_map/ppermute | solution.py:287
  26.6 23.5 %collective-permute-start.5 = (f32[584,128]{1,0:T(8,128)S(1)}, f32[584,128]{1,0:T(8,128)S(1)}, u32[]{:S(2)}, u32[]{:S(2)}) collective-permute-start(f32[584,128]{1,0:T(8,128)S(1)} %get-tuple-element.65), channel_id=1, source_target_pairs={{0,1},{1,2},{2,3},{3,4},{4,5},{5,6},{6,7},{7,8},{8,9},{9,10},{10,1... | collective-permute-start | bytes 897032 | tf_op jit(solution)/shard_map/ppermute | solution.py:290
  30.3 30.9 %collective-permute-start.4 = (f32[584,128]{1,0:T(8,128)S(1)}, f32[584,128]{1,0:T(8,128)S(1)}, u32[]{:S(2)}, u32[]{:S(2)}) collective-permute-start(f32[584,128]{1,0:T(8,128)S(1)} %get-tuple-element.64), channel_id=1, source_target_pairs={{0,1},{1,2},{2,3},{3,4},{4,5},{5,6},{6,7},{7,8},{8,9},{9,10},{10,1... | collective-permute-start | bytes 897032 | tf_op jit(solution)/shard_map/ppermute | solution.py:290
  35.1 0.7 copy-start.1
  37.5 31.4 %collective-permute-start.6 = (f32[456,128]{1,0:T(8,128)S(1)}, f32[456,128]{1,0:T(8,128)S(1)}, u32[]{:S(2)}, u32[]{:S(2)}) collective-permute-start(f32[456,128]{1,0:T(8,128)S(1)} %get-tuple-element.68), channel_id=1, source_target_pairs={{0,386},{1,387},{2,384},{3,385},{4,390},{5,391},{6,388},{7,389},{8... | collective-permute-start | bytes 700424 | tf_op jit(solution)/shard_map/ppermute | solution.py:287
  40.5 38.0 %collective-permute-start.3 = (f32[456,128]{1,0:T(8,128)S(1)}, f32[456,128]{1,0:T(8,128)S(1)}, u32[]{:S(2)}, u32[]{:S(2)}) collective-permute-start(f32[456,128]{1,0:T(8,128)S(1)} %collective-permute-done.2.refs_1_), channel_id=1, source_target_pairs={{386,1},{387,2},{384,3},{385,4},{390,5},{391,6},{388,7},{389,8},{3... | collective-permute-start | bytes 700424 | tf_op jit(solution)/shard_map/ppermute | solution.py:288
  51.0 38.0 %collective-permute-start.9 = (f32[584,128]{1,0:T(8,128)S(1)}, f32[584,128]{1,0:T(8,128)S(1)}, u32[]{:S(2)}, u32[]{:S(2)}) collective-permute-start(f32[584,128]{1,0:T(8,128)S(1)} %get-tuple-element.74), channel_id=1, source_target_pairs={{0,1},{1,2},{2,3},{3,4},{4,5},{5,6},{6,7},{7,8},{8,9},{9,10},{10,1... | collective-permute-start | bytes 897032 | tf_op jit(solution)/shard_map/ppermute | solution.py:290
  61.9 29.8 %collective-permute-start.8 = (f32[584,128]{1,0:T(8,128)S(1)}, f32[584,128]{1,0:T(8,128)S(1)}, u32[]{:S(2)}, u32[]{:S(2)}) collective-permute-start(f32[584,128]{1,0:T(8,128)S(1)} %get-tuple-element.73), channel_id=1, source_target_pairs={{0,1},{1,2},{2,3},{3,4},{4,5},{5,6},{6,7},{7,8},{8,9},{9,10},{10,1... | collective-permute-start | bytes 897032 | tf_op jit(solution)/shard_map/ppermute | solution.py:290
  68.8 27.2 %collective-permute-start.7 = (f32[456,128]{1,0:T(8,128)S(1)}, f32[456,128]{1,0:T(8,128)S(1)}, u32[]{:S(2)}, u32[]{:S(2)}) collective-permute-start(f32[456,128]{1,0:T(8,128)S(1)} %collective-permute-done.6.refs_1_), channel_id=1, source_target_pairs={{386,1},{387,2},{384,3},{385,4},{390,5},{391,6},{388,7},{389,8},{3... | collective-permute-start | bytes 700424 | tf_op jit(solution)/shard_map/ppermute | solution.py:288
  79.3 17.5 %collective-permute-start.10 = (f32[456,128]{1,0:T(8,128)S(1)}, f32[456,128]{1,0:T(8,128)S(1)}, u32[]{:S(2)}, u32[]{:S(2)}) collective-permute-start(f32[456,128]{1,0:T(8,128)S(1)} %get-tuple-element.78), channel_id=1, source_target_pairs={{0,1},{1,2},{2,3},{3,4},{4,5},{5,6},{6,7},{7,8},{8,9},{9,10},{10,1... | collective-permute-start | bytes 700424 | tf_op jit(solution)/shard_map/ppermute | solution.py:290
  89.7 15.2 %collective-permute-start.13 = (f32[584,128]{1,0:T(8,128)S(1)}, f32[584,128]{1,0:T(8,128)S(1)}, u32[]{:S(2)}, u32[]{:S(2)}) collective-permute-start(f32[584,128]{1,0:T(8,128)S(1)} %get-tuple-element.84), channel_id=1, source_target_pairs={{0,48},{1,49},{2,50},{3,51},{4,52},{5,53},{6,54},{7,55},{8,56},{9,... | collective-permute-start | bytes 897032 | tf_op jit(solution)/shard_map/ppermute | solution.py:285
  92.4 12.5 %collective-permute-start.14 = (f32[584,128]{1,0:T(8,128)S(1)}, f32[584,128]{1,0:T(8,128)S(1)}, u32[]{:S(2)}, u32[]{:S(2)}) collective-permute-start(f32[584,128]{1,0:T(8,128)S(1)} %get-tuple-element.85), channel_id=1, source_target_pairs={{0,48},{1,49},{2,50},{3,51},{4,52},{5,53},{6,54},{7,55},{8,56},{9,... | collective-permute-start | bytes 897032 | tf_op jit(solution)/shard_map/ppermute | solution.py:285
  97.6 9.5 %collective-permute-start.12 = (f32[456,128]{1,0:T(8,128)S(1)}, f32[456,128]{1,0:T(8,128)S(1)}, u32[]{:S(2)}, u32[]{:S(2)}) collective-permute-start(f32[456,128]{1,0:T(8,128)S(1)} %get-tuple-element.83), channel_id=1, source_target_pairs={{0,48},{1,49},{2,50},{3,51},{4,52},{5,53},{6,54},{7,55},{8,56},{9,... | collective-permute-start | bytes 700424 | tf_op jit(solution)/shard_map/ppermute | solution.py:285
  99.5 10.1 %collective-permute-start.11 = (f32[456,128]{1,0:T(8,128)S(1)}, f32[456,128]{1,0:T(8,128)S(1)}, u32[]{:S(2)}, u32[]{:S(2)}) collective-permute-start(f32[456,128]{1,0:T(8,128)S(1)} %get-tuple-element.82), channel_id=1, source_target_pairs={{0,48},{1,49},{2,50},{3,51},{4,52},{5,53},{6,54},{7,55},{8,56},{9,... | collective-permute-start | bytes 700424 | tf_op jit(solution)/shard_map/ppermute | solution.py:285

commit v5 on v4

--- a/solution.py
+++ b/solution.py
@@ -12,8 +12,8 @@
 Y_HI, Y_LO = 4, 2
 LANES = 128
 STATES = 8
-CHUNKS = ((0, 56, False, True), (56, 56, True, False), (112, 72, False, False), (184, 72, False, False))
-ORDERS = ((0, 1, 2, 3), (0, 2, 3, 1), (2, 3, 0, 1))
+CHUNKS = ((0, 64, False, True), (64, 56, True, False), (120, 72, False, False), (192, 64, False, False))
+ORDERS = (((0,), (1,), (2,), (3,)), ((0,), (2,), (3,), (1,)), ((2, 3), (0, 1)))
 RELAYS = {(1, 2): ((0, 1),), (1, 1): ((1, 0),)}
 LIMIT = 40 << 20
 HBM = pl.BlockSpec(memory_space=pltpu.HBM)
@@ -177,35 +177,39 @@
     )(rows_b, *kept, *after)
 
 
-def meet_kernel(first, step, edges, rows_ref, block_ref, source_ref, target_ref, *refs):
-    new_ref, grad_ref = refs[-2:]
-    size = grad_ref.shape[0]
-    counts = edge_counts(source_ref, target_ref, step, edges, first, size, rows_ref.shape[0])
-    state_row = unpack_states(block_ref, rows_ref.shape[0])
-    update_chunk(first, rows_ref[...], unpack(block_ref, size), state_row, counts, new_ref, grad_ref)
-
-
-def meet(rows_b, block, source, target, after, first, size, step):
+def meet_kernel(group, step, edges, rows_ref, *refs):
+    blocks, (source_ref, target_ref), (new_ref, grad_ref) = refs[: len(group)], refs[len(group) :][:2], refs[-2:]
+    first, size, count = group[0][0], grad_ref.shape[0], rows_ref.shape[0]
+    counts = edge_counts(source_ref, target_ref, step, edges, first, size, count)
+    parts = [unpack(ref, n) for ref, (_, n, *_) in zip(blocks, group, strict=True)]
+    state_row = sum(unpack_states(ref, count) for ref in blocks)
+    block = parts[0] if len(parts) == 1 else jnp.concatenate(parts, axis=0)
+    update_chunk(first, rows_ref[...], block, state_row, counts, new_ref, grad_ref)
+
+
+def meet(group, rows_b, blocks, source, target, after, step):
     count, width = rows_b.shape
+    size = sum(n for _, n, *_ in group)
     out = chunk_outs(size, count, width)
     return pl.pallas_call(
-        functools.partial(meet_kernel, first, step, source.shape[1] // ROUNDS),
+        functools.partial(meet_kernel, group, step, source.shape[1] // ROUNDS),
         out_shape=out,
-        in_specs=[VMEM] * 4 + [pl.BlockSpec(memory_space=pl.ANY)] * len(after),
+        in_specs=[VMEM] * (3 + len(blocks)) + [pl.BlockSpec(memory_space=pl.ANY)] * len(after),
         out_specs=[VMEM] * len(out),
         cost_estimate=chunk_cost(size, count, width),
         compiler_params=pltpu.CompilerParams(vmem_limit_bytes=LIMIT),
-    )(rows_b, block, source, target, *after)
-
-
-def bucket_kernel(fresh, rows_ref, state_ref, *refs):
+    )(rows_b, *blocks, source, target, *after)
+
+
+def bucket_kernel(begins, fresh, rows_ref, state_ref, *refs):
     pieces = len(CHUNKS)
     grads, blocks = refs[:pieces], refs[pieces : 2 * pieces]
     new_ref, new_state_ref, *rounded = refs[-2:] if refs[-1].dtype == jnp.float32 else refs[-3:]
     rows_grad = 0.0
-    for (first, size, *_), grad_ref, block_ref in zip(CHUNKS, grads, blocks, strict=True):
+    for (first, size, *_), begin, grad_ref, block_ref in zip(CHUNKS, begins, grads, blocks, strict=True):
         block = block_ref[pl.ds(first, size), :] if fresh else unpack(block_ref, size)
-        rows_grad = rows_grad + dot(grad_ref[...], block.astype(jnp.bfloat16), ((0,), (0,)))
+        grad = grad_ref[pl.ds(begin, size), :]
+        rows_grad = rows_grad + dot(grad, block.astype(jnp.bfloat16), ((0,), (0,)))
     total = state_ref.shape[1]
     mine = own_rows(0, total, total)
     state = jnp.sum(jnp.where(mine, state_ref[...], 0.0), axis=1, keepdims=True)
@@ -217,13 +221,13 @@
     new_state_ref[...] = jnp.sum(jnp.where(mine, state, 0.0), axis=0, keepdims=True)
 
 
-def update_bucket(rows, state, grads, blocks, after, fresh, last):
+def update_bucket(rows, state, grads, begins, blocks, after, fresh, last):
     count, width = rows.shape
     out = [jax.ShapeDtypeStruct(rows.shape, jnp.float32), jax.ShapeDtypeStruct(state.shape, jnp.float32)]
     if not last:
         out.append(jax.ShapeDtypeStruct(rows.shape, jnp.bfloat16))
     return pl.pallas_call(
-        functools.partial(bucket_kernel, fresh),
+        functools.partial(bucket_kernel, begins, fresh),
         out_shape=out,
         in_specs=[VMEM] * (2 + 2 * len(grads)) + [pl.BlockSpec(memory_space=pl.ANY)] * len(after),
         out_specs=[VMEM] * len(out),
@@ -234,19 +238,19 @@
     )(rows, state, *grads, *blocks, *after)
 
 
-def join_kernel(*refs):
+def join_kernel(chunks, *refs):
     blocks, (out_ref, state_ref) = refs[:-2], refs[-2:]
     total = state_ref.shape[1]
     states = 0.0
-    for (first, size, *_), block_ref in zip(CHUNKS, blocks, strict=True):
+    for (first, size), block_ref in zip(chunks, blocks, strict=True):
         out_ref[pl.ds(first, size), :] = unpack(block_ref, size)
         states = states + unpack_states(block_ref, total)
     state_ref[...] = states
 
 
-def join(blocks, count, width):
-    return pl.pallas_call(
-        join_kernel,
+def join(chunks, blocks, count, width):
+    return pl.pallas_call(
+        functools.partial(join_kernel, chunks),
         out_shape=[jax.ShapeDtypeStruct((count, width), jnp.float32), jax.ShapeDtypeStruct((1, count), jnp.float32)],
         in_specs=[VMEM] * len(blocks),
         out_specs=[VMEM] * 2,
@@ -265,35 +269,39 @@
     legs = {}
     for step in range(ROUNDS):
         last = step == ROUNDS - 1
-        moved, grads, previous = {}, {}, []
+        moved, grads, begins, previous = {}, {}, {}, []
         if step == 0:
-            front, *others = ORDERS[0]
+            (front,), *others = ORDERS[0]
+            others = [k for (k,) in others]
             new, grad, rows_b, *kept = meet_first(*whole, *CHUNKS[front][:2])
             new, grad, signal = lax.optimization_barrier((new, grad, signal))
             pairs = meet_rest([CHUNKS[k] for k in others], rows_b, kept, [grad, signal])
             met = {front: (new, grad)} | {k: tuple(pairs[2 * j : 2 * j + 2]) for j, k in enumerate(others)}
             blocks, source, target = [kept[0]] * len(CHUNKS), *kept[2:]
-        for k in ORDERS[step]:
-            first, size, *long_way = CHUNKS[k]
+        for group in ORDERS[step]:
+            k, chunks = group[0], [CHUNKS[j] for j in group]
             after = previous + [legs[at] for at in RELAYS.get((step, k), ())]
             if step == 0:
                 new, grad = met[k]
             else:
-                new, grad = meet(rows_b, blocks[k], source, target, after, first, size, step)
-            previous, grads[k] = [grad], grad
+                new, grad = meet(chunks, rows_b, [blocks[j] for j in group], source, target, after, step)
+            previous = [grad]
+            for place, j in enumerate(group):
+                grads[j], begins[j] = grad, sum(n for _, n, *_ in chunks[:place])
             if last:
-                moved[k] = lax.ppermute(new, BOTH, step_outer(*places))
-            elif long_way[step]:
+                moved[chunks[0][0], sum(n for _, n, *_ in chunks)] = lax.ppermute(new, BOTH, step_outer(*places))
+            elif chunks[0][2 + step]:
                 legs[step, k] = lax.ppermute(new, BOTH, list(relays.items()))
                 moved[k] = lax.ppermute(legs[step, k], BOTH, [(relays[p], q) for p, q in direct])
             else:
                 moved[k] = lax.ppermute(new, BOTH, direct)
         after = [legs[at] for at in RELAYS.get((step, None), ())]
-        grads = [grads[k] for k in range(len(CHUNKS))]
-        rows, row_state, *more = update_bucket(rows, row_state, grads, blocks, after, step == 0, last)
-        rows_b = more[0] if more else None
-        blocks = [moved[k] for k in range(len(CHUNKS))]
-    block, state = join(blocks, count, width)
+        grads, begins = ([table[k] for k in range(len(CHUNKS))] for table in (grads, begins))
+        rows, row_state, *more = update_bucket(rows, row_state, grads, begins, blocks, after, step == 0, last)
+        if not last:
+            rows_b = more[0]
+            blocks = [moved[k] for k in range(len(CHUNKS))]
+    block, state = join(list(moved), list(moved.values()), count, width)
     return rows, row_state.reshape(-1), block, state.reshape(-1)
 
 

time: 111 us -> 111 us (level)
  waiting for transfers between devices: 28.7 us -> 42.5 us
  starting transfers between devices: 65.7 us -> 53.7 us
  Pallas kernels: 14.6 us -> 13.1 us
    ppermute x6, starting transfers between devices: 34.7 us -> 27.5 us  [body(): moved[k] = lax.ppermute(new, BOTH, direct)]
    ppermute x4 -> x2, starting transfers between devices: 10.9 us -> 3.84 us  [body(): lax.ppermute(new, BOTH, step_outer(*places))]
    ppermute x2, waiting for transfers between devices: 6.38 us -> 13 us  [body(): lax.ppermute(legs[step, k], BOTH, [(relays[p], q) for p, q in direct])]
    ppermute x4 -> x2, waiting for transfers between devices: 4.64 us -> 8.49 us  [body(): lax.ppermute(new, BOTH, step_outer(*places))]
    ppermute x6, waiting for transfers between devices: 5.24 us -> 8.77 us  [body(): moved[k] = lax.ppermute(new, BOTH, direct)]
    pallas_call x12 -> x10, Pallas kernels: 10.9 us -> 9.43 us  [the longest x6 4.67 us: meet(): pl.pallas_call(functools.partial(meet_kernel, group, step, source.shape[1...]
    ppermute x2, starting transfers between devices: 5.83 us -> 7.21 us  [body(): legs[step, k] = lax.ppermute(new, BOTH, list(relays.items()))]
  transfers between devices with their start and end apart: 15 -> 13, of which waited for: 6 -> 7; matrix products, arithmetic and copies ran while one was open for 0% -> 0% of each run, Pallas kernels for 12% -> 11%
where the time goes in v5:
time: 111 us
  starting transfers between devices  53.7 us (48%)
  waiting for transfers between devices  42.5 us (38%)
  Pallas kernels  13.1 us (12%)
    ppermute x6, starting transfers between devices, body(): moved[k] = lax.ppermute(new, BOTH, direct)  27.5 us
    ppermute x2, starting transfers between devices, body(): lax.ppermute(legs[step, k], BOTH, [(relays[p], q) for p, q in direct])  13.9 us
    ppermute x2, waiting for transfers between devices, body(): lax.ppermute(legs[step, k], BOTH, [(relays[p], q) for p, q in direct])  13 us
    ppermute x1, waiting for transfers between devices, body(): signal = lax.ppermute(vertex_state, BOTH, mirror(*places))  12.2 us
    ppermute x6, waiting for transfers between devices, body(): moved[k] = lax.ppermute(new, BOTH, direct)  8.77 us
    ppermute x2, waiting for transfers between devices, body(): lax.ppermute(new, BOTH, step_outer(*places))  8.49 us
    ppermute x2, starting transfers between devices, body(): legs[step, k] = lax.ppermute(new, BOTH, list(relays.items()))  7.21 us
    pallas_call x6, Pallas kernels, meet(): pl.pallas_call(functools.partial(meet_kernel, group, step, source.shape[1...  4.67 us
  transfers between devices with their start and end apart: 13, of which 7 were waited for; matrix products, arithmetic and copies ran while one was open for 0% of the time, Pallas kernels for 11%

profile of v5, /device:TPU:16, one launch (start us, length us, event | category | flops | bytes accessed | tf_op | source)
XLA Modules:
  0.0 110.9 jit_solution(866504437925203322)
XLA Ops:
  0.6 1.3 %collective-permute-start = (f32[256]{0:T(256)}, f32[256]{0:T(256)S(1)}, u32[]{:S(2)}, u32[]{:S(2)}) collective-permute-start(f32[256]{0:T(256)} %param.7), channel_id=1, source_target_pairs={{24,20},{25,21},{26,22},{27,23},{28,16},{29,17},{30,18},{31,19},{3... | collective-permute-start | bytes 3080 | tf_op jit(solution)/shard_map/ppermute | solution.py:268
  1.9 2.1 %shard_map.93 = (f32[520,128]{1,0:T(8,128)S(1)}, bf16[64,256]{1,0:T(8,128)(2,1)S(1)}, bf16[256,1024]{1,0:T(8,128)(2,1)S(1)}, f32[256,1024]{1,0:T(8,128)S(1)}, f3...) custom-call(f32[256,1024]{1,0:T(8,128)} %rows_ref.1, f32[256,1024]{1,0:T(8,128)} %block_hbm.1, ...), custom_call_target="tpu_custom_call" | custom-call | flops 67108864 | bytes 524288 | tf_op jit(solution)/shard_map/pallas_call | solution.py:156
  4.1 0.0 copy-start
  4.1 12.2 %collective-permute-done.refs_1_ = f32[256]{0:T(256)S(1)} collective-permute-done((f32[256]{0:T(256)}, f32[256]{0:T(256)S(1)}, u32[]{:S(2)}, u32[]{:S(2)}) %collective-permute-start) | collective-permute-done | bytes 1056 | tf_op jit(solution)/shard_map/ppermute | solution.py:268
  16.3 5.7 %collective-permute-start.1 = (f32[520,128]{1,0:T(8,128)S(1)}, f32[520,128]{1,0:T(8,128)S(1)}, u32[]{:S(2)}, u32[]{:S(2)}) collective-permute-start(f32[520,128]{1,0:T(8,128)S(1)} %get-tuple-element.57), channel_id=1, source_target_pairs={{0,1},{1,2},{2,3},{3,4},{4,5},{5,6},{6,7},{7,8},{8,9},{9,10},{10,1... | collective-permute-start | bytes 798728 | tf_op jit(solution)/shard_map/ppermute | solution.py:297
  22.1 1.5 %shard_map.94 = (f32[456,128]{1,0:T(8,128)S(1)}, bf16[56,256]{1,0:T(8,128)(2,1)S(1)}, f32[584,128]{1,0:T(8,128)S(1)}, bf16[72,256]{1,0:T(8,128)(2,1)S(1)}, f32[5...) custom-call(bf16[256,1024]{1,0:T(8,128)(2,1)S(1)} %get-tuple-element.45.rows_ref, ...), custom_call_target="tpu_custom_call" | custom-call | flops 201326592 | bytes 1572864 | tf_op jit(solution)/shard_map/pallas_call | solution.py:170
  23.6 3.0 %collective-permute-start.2 = (f32[456,128]{1,0:T(8,128)S(1)}, f32[456,128]{1,0:T(8,128)S(1)}, u32[]{:S(2)}, u32[]{:S(2)}) collective-permute-start(f32[456,128]{1,0:T(8,128)S(1)} %get-tuple-element.59), channel_id=1, source_target_pairs={{0,386},{1,387},{2,384},{3,385},{4,390},{5,391},{6,388},{7,389},{8... | collective-permute-start | bytes 700424 | tf_op jit(solution)/shard_map/ppermute | solution.py:294
  26.6 3.6 %collective-permute-start.5 = (f32[584,128]{1,0:T(8,128)S(1)}, f32[584,128]{1,0:T(8,128)S(1)}, u32[]{:S(2)}, u32[]{:S(2)}) collective-permute-start(f32[584,128]{1,0:T(8,128)S(1)} %get-tuple-element.61), channel_id=1, source_target_pairs={{0,1},{1,2},{2,3},{3,4},{4,5},{5,6},{6,7},{7,8},{8,9},{9,10},{10,1... | collective-permute-start | bytes 897032 | tf_op jit(solution)/shard_map/ppermute | solution.py:297
  30.2 4.8 %collective-permute-start.4 = (f32[520,128]{1,0:T(8,128)S(1)}, f32[520,128]{1,0:T(8,128)S(1)}, u32[]{:S(2)}, u32[]{:S(2)}) collective-permute-start(f32[520,128]{1,0:T(8,128)S(1)} %get-tuple-element.60), channel_id=1, source_target_pairs={{0,1},{1,2},{2,3},{3,4},{4,5},{5,6},{6,7},{7,8},{8,9},{9,10},{10,1... | collective-permute-start | bytes 798728 | tf_op jit(solution)/shard_map/ppermute | solution.py:297
  35.1 0.0 copy-start.1
  35.1 0.0 copy-done
  35.1 0.7 copy-done.1
  35.7 0.9 shard_map.95
  36.7 0.0 collective-permute-done.1.refs_0_.refs_4_
  36.7 0.8 shard_map.96
  37.5 4.2 %collective-permute-start.6 = (f32[520,128]{1,0:T(8,128)S(1)}, f32[520,128]{1,0:T(8,128)S(1)}, u32[]{:S(2)}, u32[]{:S(2)}) collective-permute-start(f32[520,128]{1,0:T(8,128)S(1)} %get-tuple-element.64), channel_id=1, source_target_pairs={{0,386},{1,387},{2,384},{3,385},{4,390},{5,391},{6,388},{7,389},{8... | collective-permute-start | bytes 798728 | tf_op jit(solution)/shard_map/ppermute | solution.py:294
  41.7 0.0 collective-permute-done.2.refs_4_
  41.7 8.5 %collective-permute-start.3 = (f32[456,128]{1,0:T(8,128)S(1)}, f32[456,128]{1,0:T(8,128)S(1)}, u32[]{:S(2)}, u32[]{:S(2)}) collective-permute-start(f32[456,128]{1,0:T(8,128)S(1)} %collective-permute-done.2.refs_4_), channel_id=1, source_target_pairs={{386,1},{387,2},{384,3},{385,4},{390,5},{391,6},{388,7},{389,8},{3... | collective-permute-start | bytes 700424 | tf_op jit(solution)/shard_map/ppermute | solution.py:295
  50.2 0.0 collective-permute-done.5.refs_0_.refs_6_
  50.2 0.8 shard_map.97
  51.0 4.6 %collective-permute-start.9 = (f32[584,128]{1,0:T(8,128)S(1)}, f32[584,128]{1,0:T(8,128)S(1)}, u32[]{:S(2)}, u32[]{:S(2)}) collective-permute-start(f32[584,128]{1,0:T(8,128)S(1)} %get-tuple-element.70), channel_id=1, source_target_pairs={{0,1},{1,2},{2,3},{3,4},{4,5},{5,6},{6,7},{7,8},{8,9},{9,10},{10,1... | collective-permute-start | bytes 897032 | tf_op jit(solution)/shard_map/ppermute | solution.py:297
  55.5 3.7 %collective-permute-done.4.refs_0_.refs_7_ = f32[520,128]{1,0:T(8,128)S(1)} collective-permute-done((f32[520,128]{1,0:T(8,128)S(1)}, f32[520,128]{1,0:T(8,128)S(1)}, u32[]{:S(2)}, u32[]{:S(2)}) %collective-permute-start.4) | collective-permute-done | bytes 266272 | tf_op jit(solution)/shard_map/ppermute | solution.py:297
  59.2 0.8 shard_map.98
  60.0 6.9 %collective-permute-start.10 = (f32[520,128]{1,0:T(8,128)S(1)}, f32[520,128]{1,0:T(8,128)S(1)}, u32[]{:S(2)}, u32[]{:S(2)}) collective-permute-start(f32[520,128]{1,0:T(8,128)S(1)} %get-tuple-element.71), channel_id=1, source_target_pairs={{0,1},{1,2},{2,3},{3,4},{4,5},{5,6},{6,7},{7,8},{8,9},{9,10},{10,1... | collective-permute-start | bytes 798728 | tf_op jit(solution)/shard_map/ppermute | solution.py:297
  66.9 0.0 collective-permute-done.6.refs_4_
  66.9 5.4 %collective-permute-start.7 = (f32[520,128]{1,0:T(8,128)S(1)}, f32[520,128]{1,0:T(8,128)S(1)}, u32[]{:S(2)}, u32[]{:S(2)}) collective-permute-start(f32[520,128]{1,0:T(8,128)S(1)} %collective-permute-done.6.refs_4_), channel_id=1, source_target_pairs={{386,1},{387,2},{384,3},{385,4},{390,5},{391,6},{388,7},{389,8},{3... | collective-permute-start | bytes 798728 | tf_op jit(solution)/shard_map/ppermute | solution.py:295
  72.3 11.7 %collective-permute-done.3.refs_0_.refs_5_ = f32[456,128]{1,0:T(8,128)S(1)} collective-permute-done((f32[456,128]{1,0:T(8,128)S(1)}, f32[456,128]{1,0:T(8,128)S(1)}, u32[]{:S(2)}, u32[]{:S(2)}) %collective-permute-start.3) | collective-permute-done | bytes 233504 | tf_op jit(solution)/shard_map/ppermute | solution.py:295
  84.0 0.8 shard_map.99
  84.8 1.9 %collective-permute-start.8 = (f32[456,128]{1,0:T(8,128)S(1)}, f32[456,128]{1,0:T(8,128)S(1)}, u32[]{:S(2)}, u32[]{:S(2)}) collective-permute-start(f32[456,128]{1,0:T(8,128)S(1)} %get-tuple-element.69), channel_id=1, source_target_pairs={{0,1},{1,2},{2,3},{3,4},{4,5},{5,6},{6,7},{7,8},{8,9},{9,10},{10,1... | collective-permute-start | bytes 700424 | tf_op jit(solution)/shard_map/ppermute | solution.py:297
  86.7 0.9 shard_map.100
  87.7 0.0 collective-permute-done.10.refs_1_.refs_7_
  87.7 0.0 collective-permute-done.9.refs_0_.refs_6_
  87.7 0.8 shard_map.101
  88.5 1.9 %collective-permute-start.11 = (f32[1096,128]{1,0:T(8,128)S(1)}, f32[1096,128]{1,0:T(8,128)S(1)}, u32[]{:S(2)}, u32[]{:S(2)}) collective-permute-start(f32[1096,128]{1,0:T(8,128)S(1)} %get-tuple-element.76), channel_id=1, source_target_pairs={{0,48},{1,49},{2,50},{3,51},{4,52},{5,53},{6,54},{7,55},{8,56},{9,... | collective-permute-start | bytes 1683464 | tf_op jit(solution)/shard_map/ppermute | solution.py:292
  90.4 5.0 %collective-permute-done.8.refs_1_.refs_5_ = f32[456,128]{1,0:T(8,128)S(1)} collective-permute-done((f32[456,128]{1,0:T(8,128)S(1)}, f32[456,128]{1,0:T(8,128)S(1)}, u32[]{:S(2)}, u32[]{:S(2)}) %collective-permute-start.8) | collective-permute-done | bytes 233504 | tf_op jit(solution)/shard_map/ppermute | solution.py:297
  95.5 1.2 %collective-permute-done.7.refs_0_.refs_4_ = f32[520,128]{1,0:T(8,128)S(1)} collective-permute-done((f32[520,128]{1,0:T(8,128)S(1)}, f32[520,128]{1,0:T(8,128)S(1)}, u32[]{:S(2)}, u32[]{:S(2)}) %collective-permute-start.7) | collective-permute-done | bytes 266272 | tf_op jit(solution)/shard_map/ppermute | solution.py:295
  96.7 0.8 shard_map.102
  97.5 1.9 %collective-permute-start.12 = (f32[968,128]{1,0:T(8,128)S(1)}, f32[968,128]{1,0:T(8,128)S(1)}, u32[]{:S(2)}, u32[]{:S(2)}) collective-permute-start(f32[968,128]{1,0:T(8,128)S(1)} %get-tuple-element.77), channel_id=1, source_target_pairs={{0,48},{1,49},{2,50},{3,51},{4,52},{5,53},{6,54},{7,55},{8,56},{9,... | collective-permute-start | bytes 1486856 | tf_op jit(solution)/shard_map/ppermute | solution.py:292
  99.4 1.9 %shard_map.103 = (f32[256,1024]{1,0:T(8,128)}, f32[1,256]{1,0:T(1,128)}) custom-call(f32[256,1024]{1,0:T(8,128)S(1)} %get-tuple-element.66.rows_ref, f32[1,256]{1,0:T(1,128)S(1)} %get-tuple-element.67.state_ref, bf16[120,256]{1,0:T(8,128)(2,1)S(1)} %get-tuple-element.73.refs_0_.refs_1_, bf16[120,256]{1,0:T(8,128)(2,1)S(1)} %get-tuple-element.73.refs_0_.refs_1_, ...), custom_call_target="tpu_custom_call" | custom-call | flops 134217728 | bytes 3145728 | tf_op jit(solution)/shard_map/pallas_call | solution.py:229
  101.3 2.5 %collective-permute-done.11.refs_0_ = f32[1096,128]{1,0:T(8,128)S(1)} collective-permute-done((f32[1096,128]{1,0:T(8,128)S(1)}, f32[1096,128]{1,0:T(8,128)S(1)}, u32[]{:S(2)}, u32[]{:S(2)}) %collective-permute-start.11) | collective-permute-done | bytes 561184 | tf_op jit(solution)/shard_map/ppermute | solution.py:292
  103.8 6.0 %collective-permute-done.12.refs_1_ = f32[968,128]{1,0:T(8,128)S(1)} collective-permute-done((f32[968,128]{1,0:T(8,128)S(1)}, f32[968,128]{1,0:T(8,128)S(1)}, u32[]{:S(2)}, u32[]{:S(2)}) %collective-permute-start.12) | collective-permute-done | bytes 495648 | tf_op jit(solution)/shard_map/ppermute | solution.py:292
  109.8 1.0 shard_map.104
Async XLA Ops:
  0.6 15.7 %collective-permute-start = (f32[256]{0:T(256)}, f32[256]{0:T(256)S(1)}, u32[]{:S(2)}, u32[]{:S(2)}) collective-permute-start(f32[256]{0:T(256)} %param.7), channel_id=1, source_target_pairs={{24,20},{25,21},{26,22},{27,23},{28,16},{29,17},{30,18},{31,19},{3... | collective-permute-start | bytes 3080 | tf_op jit(solution)/shard_map/ppermute | solution.py:268
  4.1 31.0 %copy-start = (f32[256,1024]{1,0:T(8,128)S(1)}, f32[256,1024]{1,0:T(8,128)}, u32[]{:S(2)}) copy-start(f32[256,1024]{1,0:T(8,128)} %rows_ref.1) | copy-start | bytes 3145732
  16.3 20.3 %collective-permute-start.1 = (f32[520,128]{1,0:T(8,128)S(1)}, f32[520,128]{1,0:T(8,128)S(1)}, u32[]{:S(2)}, u32[]{:S(2)}) collective-permute-start(f32[520,128]{1,0:T(8,128)S(1)} %get-tuple-element.57), channel_id=1, source_target_pairs={{0,1},{1,2},{2,3},{3,4},{4,5},{5,6},{6,7},{7,8},{8,9},{9,10},{10,1... | collective-permute-start | bytes 798728 | tf_op jit(solution)/shard_map/ppermute | solution.py:297
  23.6 18.1 %collective-permute-start.2 = (f32[456,128]{1,0:T(8,128)S(1)}, f32[456,128]{1,0:T(8,128)S(1)}, u32[]{:S(2)}, u32[]{:S(2)}) collective-permute-start(f32[456,128]{1,0:T(8,128)S(1)} %get-tuple-element.59), channel_id=1, source_target_pairs={{0,386},{1,387},{2,384},{3,385},{4,390},{5,391},{6,388},{7,389},{8... | collective-permute-start | bytes 700424 | tf_op jit(solution)/shard_map/ppermute | solution.py:294
  26.6 23.6 %collective-permute-start.5 = (f32[584,128]{1,0:T(8,128)S(1)}, f32[584,128]{1,0:T(8,128)S(1)}, u32[]{:S(2)}, u32[]{:S(2)}) collective-permute-start(f32[584,128]{1,0:T(8,128)S(1)} %get-tuple-element.61), channel_id=1, source_target_pairs={{0,1},{1,2},{2,3},{3,4},{4,5},{5,6},{6,7},{7,8},{8,9},{9,10},{10,1... | collective-permute-start | bytes 897032 | tf_op jit(solution)/shard_map/ppermute | solution.py:297
  30.2 29.0 %collective-permute-start.4 = (f32[520,128]{1,0:T(8,128)S(1)}, f32[520,128]{1,0:T(8,128)S(1)}, u32[]{:S(2)}, u32[]{:S(2)}) collective-permute-start(f32[520,128]{1,0:T(8,128)S(1)} %get-tuple-element.60), channel_id=1, source_target_pairs={{0,1},{1,2},{2,3},{3,4},{4,5},{5,6},{6,7},{7,8},{8,9},{9,10},{10,1... | collective-permute-start | bytes 798728 | tf_op jit(solution)/shard_map/ppermute | solution.py:297
  35.1 0.7 copy-start.1
  37.5 29.4 %collective-permute-start.6 = (f32[520,128]{1,0:T(8,128)S(1)}, f32[520,128]{1,0:T(8,128)S(1)}, u32[]{:S(2)}, u32[]{:S(2)}) collective-permute-start(f32[520,128]{1,0:T(8,128)S(1)} %get-tuple-element.64), channel_id=1, source_target_pairs={{0,386},{1,387},{2,384},{3,385},{4,390},{5,391},{6,388},{7,389},{8... | collective-permute-start | bytes 798728 | tf_op jit(solution)/shard_map/ppermute | solution.py:294
  41.7 42.4 %collective-permute-start.3 = (f32[456,128]{1,0:T(8,128)S(1)}, f32[456,128]{1,0:T(8,128)S(1)}, u32[]{:S(2)}, u32[]{:S(2)}) collective-permute-start(f32[456,128]{1,0:T(8,128)S(1)} %collective-permute-done.2.refs_4_), channel_id=1, source_target_pairs={{386,1},{387,2},{384,3},{385,4},{390,5},{391,6},{388,7},{389,8},{3... | collective-permute-start | bytes 700424 | tf_op jit(solution)/shard_map/ppermute | solution.py:295
  51.0 36.7 %collective-permute-start.9 = (f32[584,128]{1,0:T(8,128)S(1)}, f32[584,128]{1,0:T(8,128)S(1)}, u32[]{:S(2)}, u32[]{:S(2)}) collective-permute-start(f32[584,128]{1,0:T(8,128)S(1)} %get-tuple-element.70), channel_id=1, source_target_pairs={{0,1},{1,2},{2,3},{3,4},{4,5},{5,6},{6,7},{7,8},{8,9},{9,10},{10,1... | collective-permute-start | bytes 897032 | tf_op jit(solution)/shard_map/ppermute | solution.py:297
  60.0 27.7 %collective-permute-start.10 = (f32[520,128]{1,0:T(8,128)S(1)}, f32[520,128]{1,0:T(8,128)S(1)}, u32[]{:S(2)}, u32[]{:S(2)}) collective-permute-start(f32[520,128]{1,0:T(8,128)S(1)} %get-tuple-element.71), channel_id=1, source_target_pairs={{0,1},{1,2},{2,3},{3,4},{4,5},{5,6},{6,7},{7,8},{8,9},{9,10},{10,1... | collective-permute-start | bytes 798728 | tf_op jit(solution)/shard_map/ppermute | solution.py:297
  66.9 29.8 %collective-permute-start.7 = (f32[520,128]{1,0:T(8,128)S(1)}, f32[520,128]{1,0:T(8,128)S(1)}, u32[]{:S(2)}, u32[]{:S(2)}) collective-permute-start(f32[520,128]{1,0:T(8,128)S(1)} %collective-permute-done.6.refs_4_), channel_id=1, source_target_pairs={{386,1},{387,2},{384,3},{385,4},{390,5},{391,6},{388,7},{389,8},{3... | collective-permute-start | bytes 798728 | tf_op jit(solution)/shard_map/ppermute | solution.py:295
  84.8 10.7 %collective-permute-start.8 = (f32[456,128]{1,0:T(8,128)S(1)}, f32[456,128]{1,0:T(8,128)S(1)}, u32[]{:S(2)}, u32[]{:S(2)}) collective-permute-start(f32[456,128]{1,0:T(8,128)S(1)} %get-tuple-element.69), channel_id=1, source_target_pairs={{0,1},{1,2},{2,3},{3,4},{4,5},{5,6},{6,7},{7,8},{8,9},{9,10},{10,1... | collective-permute-start | bytes 700424 | tf_op jit(solution)/shard_map/ppermute | solution.py:297
  88.5 15.3 %collective-permute-start.11 = (f32[1096,128]{1,0:T(8,128)S(1)}, f32[1096,128]{1,0:T(8,128)S(1)}, u32[]{:S(2)}, u32[]{:S(2)}) collective-permute-start(f32[1096,128]{1,0:T(8,128)S(1)} %get-tuple-element.76), channel_id=1, source_target_pairs={{0,48},{1,49},{2,50},{3,51},{4,52},{5,53},{6,54},{7,55},{8,56},{9,... | collective-permute-start | bytes 1683464 | tf_op jit(solution)/shard_map/ppermute | solution.py:292
  97.5 12.3 %collective-permute-start.12 = (f32[968,128]{1,0:T(8,128)S(1)}, f32[968,128]{1,0:T(8,128)S(1)}, u32[]{:S(2)}, u32[]{:S(2)}) collective-permute-start(f32[968,128]{1,0:T(8,128)S(1)} %get-tuple-element.77), channel_id=1, source_target_pairs={{0,48},{1,49},{2,50},{3,51},{4,52},{5,53},{6,54},{7,55},{8,56},{9,... | collective-permute-start | bytes 1486856 | tf_op jit(solution)/shard_map/ppermute | solution.py:292

commit v6 on v4

--- a/solution.py
+++ b/solution.py
@@ -10,6 +10,7 @@
 ROUNDS = 3
 BOTH = ("outer", "inner")
 Y_HI, Y_LO = 4, 2
+LEAD = 1
 LANES = 128
 STATES = 8
 CHUNKS = ((0, 56, False, True), (56, 56, True, False), (112, 72, False, False), (184, 72, False, False))
@@ -39,11 +40,11 @@
 
 
 def mirror(n_outer, n_inner):
-    n_z = n_inner // Y_HI
+    top = n_inner // Y_HI - 1 - LEAD
     return [
-        (o * n_inner + z * Y_HI + y, o * n_inner + (n_z - 1 - z) * Y_HI + y)
+        (o * n_inner + (top - z) * Y_HI + y, o * n_inner + z * Y_HI + y)
         for o in range(n_outer)
-        for z in range((n_z + 1) // 2, n_z)
+        for z in range((top + 1) // 2)
         for y in range(Y_HI)
     ]
 

time: 111 us -> 111 us (level)
  starting transfers between devices: 65.7 us -> 63.6 us
  waiting for transfers between devices: 28.7 us -> 30.5 us
    ppermute x6, starting transfers between devices: 34.7 us -> 32.8 us  [body(): moved[k] = lax.ppermute(new, BOTH, direct)]
    ppermute x2, waiting for transfers between devices: 6.38 us -> 8.02 us  [body(): lax.ppermute(legs[step, k], BOTH, [(relays[p], q) for p, q in direct])]
where the time goes in v6:
time: 111 us; the launch traced here: 110 us
  starting transfers between devices  63.6 us (57%)
  waiting for transfers between devices  30.5 us (27%)
  Pallas kernels  14.6 us (13%)
    ppermute x6, starting transfers between devices, body(): moved[k] = lax.ppermute(new, BOTH, direct)  32.8 us
    ppermute x2, starting transfers between devices, body(): lax.ppermute(legs[step, k], BOTH, [(relays[p], q) for p, q in direct])  13 us
    ppermute x1, waiting for transfers between devices, body(): signal = lax.ppermute(vertex_state, BOTH, mirror(*places))  12.2 us
    ppermute x4, starting transfers between devices, body(): moved[k] = lax.ppermute(new, BOTH, step_outer(*places))  10.8 us
    ppermute x2, waiting for transfers between devices, body(): lax.ppermute(legs[step, k], BOTH, [(relays[p], q) for p, q in direct])  8.02 us
    pallas_call x8, Pallas kernels, meet(): pl.pallas_call(functools.partial(meet_kernel, first, step, source.shape[1...  6.11 us
    ppermute x2, starting transfers between devices, body(): legs[step, k] = lax.ppermute(new, BOTH, list(relays.items()))  5.82 us
    ppermute x6, waiting for transfers between devices, body(): moved[k] = lax.ppermute(new, BOTH, direct)  5.22 us
  transfers between devices with their start and end apart: 15, of which 6 were waited for; matrix products, arithmetic and copies ran while one was open for 0% of the time, Pallas kernels for 12%

profile of v6, /device:TPU:16, one launch (start us, length us, event | category | flops | bytes accessed | tf_op | source)
XLA Modules:
  0.0 110.3 jit_solution(2319902550341876997)
XLA Ops:
  0.6 1.3 %collective-permute-start = (f32[256]{0:T(256)}, f32[256]{0:T(256)S(1)}, u32[]{:S(2)}, u32[]{:S(2)}) collective-permute-start(f32[256]{0:T(256)} %param.7), channel_id=1, source_target_pairs={{40,0},{41,1},{42,2},{43,3},{36,4},{37,5},{38,6},{39,7},{32,8},{33... | collective-permute-start | bytes 3080 | tf_op jit(solution)/shard_map/ppermute | solution.py:265
  1.9 2.1 %shard_map.93 = (f32[456,128]{1,0:T(8,128)S(1)}, bf16[56,256]{1,0:T(8,128)(2,1)S(1)}, bf16[256,1024]{1,0:T(8,128)(2,1)S(1)}, f32[256,1024]{1,0:T(8,128)S(1)}, f3...) custom-call(f32[256,1024]{1,0:T(8,128)} %rows_ref.1, f32[256,1024]{1,0:T(8,128)} %block_hbm.1, ...), custom_call_target="tpu_custom_call" | custom-call | flops 58720256 | bytes 458752 | tf_op jit(solution)/shard_map/pallas_call | solution.py:157
  4.1 0.0 copy-start
  4.1 12.2 %collective-permute-done.refs_1_ = f32[256]{0:T(256)S(1)} collective-permute-done((f32[256]{0:T(256)}, f32[256]{0:T(256)S(1)}, u32[]{:S(2)}, u32[]{:S(2)}) %collective-permute-start) | collective-permute-done | bytes 1056 | tf_op jit(solution)/shard_map/ppermute | solution.py:265
  16.3 5.7 %collective-permute-start.1 = (f32[456,128]{1,0:T(8,128)S(1)}, f32[456,128]{1,0:T(8,128)S(1)}, u32[]{:S(2)}, u32[]{:S(2)}) collective-permute-start(f32[456,128]{1,0:T(8,128)S(1)} %get-tuple-element.61), channel_id=1, source_target_pairs={{0,1},{1,2},{2,3},{3,4},{4,5},{5,6},{6,7},{7,8},{8,9},{9,10},{10,1... | collective-permute-start | bytes 700424 | tf_op jit(solution)/shard_map/ppermute | solution.py:291
  22.0 1.6 %shard_map.94 = (f32[456,128]{1,0:T(8,128)S(1)}, bf16[56,256]{1,0:T(8,128)(2,1)S(1)}, f32[584,128]{1,0:T(8,128)S(1)}, bf16[72,256]{1,0:T(8,128)(2,1)S(1)}, f32[5...) custom-call(bf16[256,1024]{1,0:T(8,128)(2,1)S(1)} %get-tuple-element.49.rows_ref, ...), custom_call_target="tpu_custom_call" | custom-call | flops 209715200 | bytes 1638400 | tf_op jit(solution)/shard_map/pallas_call | solution.py:171
  23.6 3.0 %collective-permute-start.2 = (f32[456,128]{1,0:T(8,128)S(1)}, f32[456,128]{1,0:T(8,128)S(1)}, u32[]{:S(2)}, u32[]{:S(2)}) collective-permute-start(f32[456,128]{1,0:T(8,128)S(1)} %get-tuple-element.63), channel_id=1, source_target_pairs={{0,386},{1,387},{2,384},{3,385},{4,390},{5,391},{6,388},{7,389},{8... | collective-permute-start | bytes 700424 | tf_op jit(solution)/shard_map/ppermute | solution.py:288
  26.6 3.6 %collective-permute-start.5 = (f32[584,128]{1,0:T(8,128)S(1)}, f32[584,128]{1,0:T(8,128)S(1)}, u32[]{:S(2)}, u32[]{:S(2)}) collective-permute-start(f32[584,128]{1,0:T(8,128)S(1)} %get-tuple-element.65), channel_id=1, source_target_pairs={{0,1},{1,2},{2,3},{3,4},{4,5},{5,6},{6,7},{7,8},{8,9},{9,10},{10,1... | collective-permute-start | bytes 897032 | tf_op jit(solution)/shard_map/ppermute | solution.py:291
  30.2 4.8 %collective-permute-start.4 = (f32[584,128]{1,0:T(8,128)S(1)}, f32[584,128]{1,0:T(8,128)S(1)}, u32[]{:S(2)}, u32[]{:S(2)}) collective-permute-start(f32[584,128]{1,0:T(8,128)S(1)} %get-tuple-element.64), channel_id=1, source_target_pairs={{0,1},{1,2},{2,3},{3,4},{4,5},{5,6},{6,7},{7,8},{8,9},{9,10},{10,1... | collective-permute-start | bytes 897032 | tf_op jit(solution)/shard_map/ppermute | solution.py:291
  35.1 0.0 copy-start.1
  35.1 0.0 copy-done
  35.1 0.7 copy-done.1
  35.7 0.9 shard_map.95
  36.7 0.0 collective-permute-done.1.block_ref.refs_4_
  36.7 0.8 shard_map.96
  37.4 2.8 %collective-permute-start.6 = (f32[456,128]{1,0:T(8,128)S(1)}, f32[456,128]{1,0:T(8,128)S(1)}, u32[]{:S(2)}, u32[]{:S(2)}) collective-permute-start(f32[456,128]{1,0:T(8,128)S(1)} %get-tuple-element.68), channel_id=1, source_target_pairs={{0,386},{1,387},{2,384},{3,385},{4,390},{5,391},{6,388},{7,389},{8... | collective-permute-start | bytes 700424 | tf_op jit(solution)/shard_map/ppermute | solution.py:288
  40.3 0.2 collective-permute-done.2.refs_1_
  40.5 9.6 %collective-permute-start.3 = (f32[456,128]{1,0:T(8,128)S(1)}, f32[456,128]{1,0:T(8,128)S(1)}, u32[]{:S(2)}, u32[]{:S(2)}) collective-permute-start(f32[456,128]{1,0:T(8,128)S(1)} %collective-permute-done.2.refs_1_), channel_id=1, source_target_pairs={{386,1},{387,2},{384,3},{385,4},{390,5},{391,6},{388,7},{389,8},{3... | collective-permute-start | bytes 700424 | tf_op jit(solution)/shard_map/ppermute | solution.py:289
  50.2 0.0 collective-permute-done.5.block_ref.refs_6_
  50.2 0.8 shard_map.97
  50.9 4.9 %collective-permute-start.9 = (f32[584,128]{1,0:T(8,128)S(1)}, f32[584,128]{1,0:T(8,128)S(1)}, u32[]{:S(2)}, u32[]{:S(2)}) collective-permute-start(f32[584,128]{1,0:T(8,128)S(1)} %get-tuple-element.74), channel_id=1, source_target_pairs={{0,1},{1,2},{2,3},{3,4},{4,5},{5,6},{6,7},{7,8},{8,9},{9,10},{10,1... | collective-permute-start | bytes 897032 | tf_op jit(solution)/shard_map/ppermute | solution.py:291
  55.8 5.2 %collective-permute-done.4.block_ref.refs_7_ = f32[584,128]{1,0:T(8,128)S(1)} collective-permute-done((f32[584,128]{1,0:T(8,128)S(1)}, f32[584,128]{1,0:T(8,128)S(1)}, u32[]{:S(2)}, u32[]{:S(2)}) %collective-permute-start.4) | collective-permute-done | bytes 299040 | tf_op jit(solution)/shard_map/ppermute | solution.py:291
  61.0 0.8 shard_map.98
  61.8 6.9 %collective-permute-start.8 = (f32[584,128]{1,0:T(8,128)S(1)}, f32[584,128]{1,0:T(8,128)S(1)}, u32[]{:S(2)}, u32[]{:S(2)}) collective-permute-start(f32[584,128]{1,0:T(8,128)S(1)} %get-tuple-element.73), channel_id=1, source_target_pairs={{0,1},{1,2},{2,3},{3,4},{4,5},{5,6},{6,7},{7,8},{8,9},{9,10},{10,1... | collective-permute-start | bytes 897032 | tf_op jit(solution)/shard_map/ppermute | solution.py:291
  68.8 0.0 collective-permute-done.6.refs_1_
  68.8 3.3 %collective-permute-start.7 = (f32[456,128]{1,0:T(8,128)S(1)}, f32[456,128]{1,0:T(8,128)S(1)}, u32[]{:S(2)}, u32[]{:S(2)}) collective-permute-start(f32[456,128]{1,0:T(8,128)S(1)} %collective-permute-done.6.refs_1_), channel_id=1, source_target_pairs={{386,1},{387,2},{384,3},{385,4},{390,5},{391,6},{388,7},{389,8},{3... | collective-permute-start | bytes 700424 | tf_op jit(solution)/shard_map/ppermute | solution.py:289
  72.1 8.0 %collective-permute-done.3.block_ref.refs_5_ = f32[456,128]{1,0:T(8,128)S(1)} collective-permute-done((f32[456,128]{1,0:T(8,128)S(1)}, f32[456,128]{1,0:T(8,128)S(1)}, u32[]{:S(2)}, u32[]{:S(2)}) %collective-permute-start.3) | collective-permute-done | bytes 233504 | tf_op jit(solution)/shard_map/ppermute | solution.py:289
  80.1 0.8 shard_map.99
  80.9 6.8 %collective-permute-start.10 = (f32[456,128]{1,0:T(8,128)S(1)}, f32[456,128]{1,0:T(8,128)S(1)}, u32[]{:S(2)}, u32[]{:S(2)}) collective-permute-start(f32[456,128]{1,0:T(8,128)S(1)} %get-tuple-element.78), channel_id=1, source_target_pairs={{0,1},{1,2},{2,3},{3,4},{4,5},{5,6},{6,7},{7,8},{8,9},{9,10},{10,1... | collective-permute-start | bytes 700424 | tf_op jit(solution)/shard_map/ppermute | solution.py:291
  87.7 0.9 shard_map.100
  88.7 0.0 collective-permute-done.9.block_ref.refs_6_
  88.7 0.8 shard_map.101
  89.5 1.9 %collective-permute-start.13 = (f32[584,128]{1,0:T(8,128)S(1)}, f32[584,128]{1,0:T(8,128)S(1)}, u32[]{:S(2)}, u32[]{:S(2)}) collective-permute-start(f32[584,128]{1,0:T(8,128)S(1)} %get-tuple-element.84), channel_id=1, source_target_pairs={{0,48},{1,49},{2,50},{3,51},{4,52},{5,53},{6,54},{7,55},{8,56},{9,... | collective-permute-start | bytes 897032 | tf_op jit(solution)/shard_map/ppermute | solution.py:286
  91.4 0.0 collective-permute-done.8.block_ref.refs_7_
  91.4 0.8 shard_map.102
  92.2 3.5 %collective-permute-start.14 = (f32[584,128]{1,0:T(8,128)S(1)}, f32[584,128]{1,0:T(8,128)S(1)}, u32[]{:S(2)}, u32[]{:S(2)}) collective-permute-start(f32[584,128]{1,0:T(8,128)S(1)} %get-tuple-element.85), channel_id=1, source_target_pairs={{0,48},{1,49},{2,50},{3,51},{4,52},{5,53},{6,54},{7,55},{8,56},{9,... | collective-permute-start | bytes 897032 | tf_op jit(solution)/shard_map/ppermute | solution.py:286
  95.7 0.0 collective-permute-done.7.block_ref.refs_4_
  95.7 0.8 shard_map.103
  96.5 0.0 collective-permute-done.10.block_ref.refs_5_
  96.5 0.8 shard_map.104
  97.2 1.9 %collective-permute-start.12 = (f32[456,128]{1,0:T(8,128)S(1)}, f32[456,128]{1,0:T(8,128)S(1)}, u32[]{:S(2)}, u32[]{:S(2)}) collective-permute-start(f32[456,128]{1,0:T(8,128)S(1)} %get-tuple-element.83), channel_id=1, source_target_pairs={{0,48},{1,49},{2,50},{3,51},{4,52},{5,53},{6,54},{7,55},{8,56},{9,... | collective-permute-start | bytes 700424 | tf_op jit(solution)/shard_map/ppermute | solution.py:286
  99.2 3.4 %collective-permute-start.11 = (f32[456,128]{1,0:T(8,128)S(1)}, f32[456,128]{1,0:T(8,128)S(1)}, u32[]{:S(2)}, u32[]{:S(2)}) collective-permute-start(f32[456,128]{1,0:T(8,128)S(1)} %get-tuple-element.82), channel_id=1, source_target_pairs={{0,48},{1,49},{2,50},{3,51},{4,52},{5,53},{6,54},{7,55},{8,56},{9,... | collective-permute-start | bytes 700424 | tf_op jit(solution)/shard_map/ppermute | solution.py:286
  102.6 1.9 %shard_map.105 = (f32[256,1024]{1,0:T(8,128)}, f32[1,256]{1,0:T(1,128)}) custom-call(f32[256,1024]{1,0:T(8,128)S(1)} %get-tuple-element.70.rows_ref, f32[1,256]{1,0:T(1,128)S(1)} %get-tuple-element.71.state_ref, bf16[56,256]{1,0:T(8,128)(2,1)S(1)} %get-tuple-element.77.refs_0_, bf16[56,256]{1,0:T(8,128)(2,1)S(1)} %get-tuple-element.79.refs_1_, ...), custom_call_target="tpu_custom_call" | custom-call | flops 134217728 | bytes 3145728 | tf_op jit(solution)/shard_map/pallas_call | solution.py:226
  104.5 0.0 collective-permute-done.13.refs_2_
  104.5 0.0 collective-permute-done.14.refs_3_
  104.5 2.2 %collective-permute-done.12.refs_1_ = f32[456,128]{1,0:T(8,128)S(1)} collective-permute-done((f32[456,128]{1,0:T(8,128)S(1)}, f32[456,128]{1,0:T(8,128)S(1)}, u32[]{:S(2)}, u32[]{:S(2)}) %collective-permute-start.12) | collective-permute-done | bytes 233504 | tf_op jit(solution)/shard_map/ppermute | solution.py:286
  106.7 2.5 %collective-permute-done.11.refs_0_ = f32[456,128]{1,0:T(8,128)S(1)} collective-permute-done((f32[456,128]{1,0:T(8,128)S(1)}, f32[456,128]{1,0:T(8,128)S(1)}, u32[]{:S(2)}, u32[]{:S(2)}) %collective-permute-start.11) | collective-permute-done | bytes 233504 | tf_op jit(solution)/shard_map/ppermute | solution.py:286
  109.2 1.0 shard_map.106
Async XLA Ops:
  0.6 15.7 %collective-permute-start = (f32[256]{0:T(256)}, f32[256]{0:T(256)S(1)}, u32[]{:S(2)}, u32[]{:S(2)}) collective-permute-start(f32[256]{0:T(256)} %param.7), channel_id=1, source_target_pairs={{40,0},{41,1},{42,2},{43,3},{36,4},{37,5},{38,6},{39,7},{32,8},{33... | collective-permute-start | bytes 3080 | tf_op jit(solution)/shard_map/ppermute | solution.py:265
  4.1 31.0 %copy-start = (f32[256,1024]{1,0:T(8,128)S(1)}, f32[256,1024]{1,0:T(8,128)}, u32[]{:S(2)}) copy-start(f32[256,1024]{1,0:T(8,128)} %rows_ref.1) | copy-start | bytes 3145732
  16.3 20.3 %collective-permute-start.1 = (f32[456,128]{1,0:T(8,128)S(1)}, f32[456,128]{1,0:T(8,128)S(1)}, u32[]{:S(2)}, u32[]{:S(2)}) collective-permute-start(f32[456,128]{1,0:T(8,128)S(1)} %get-tuple-element.61), channel_id=1, source_target_pairs={{0,1},{1,2},{2,3},{3,4},{4,5},{5,6},{6,7},{7,8},{8,9},{9,10},{10,1... | collective-permute-start | bytes 700424 | tf_op jit(solution)/shard_map/ppermute | solution.py:291
  23.6 16.9 %collective-permute-start.2 = (f32[456,128]{1,0:T(8,128)S(1)}, f32[456,128]{1,0:T(8,128)S(1)}, u32[]{:S(2)}, u32[]{:S(2)}) collective-permute-start(f32[456,128]{1,0:T(8,128)S(1)} %get-tuple-element.63), channel_id=1, source_target_pairs={{0,386},{1,387},{2,384},{3,385},{4,390},{5,391},{6,388},{7,389},{8... | collective-permute-start | bytes 700424 | tf_op jit(solution)/shard_map/ppermute | solution.py:288
  26.6 23.5 %collective-permute-start.5 = (f32[584,128]{1,0:T(8,128)S(1)}, f32[584,128]{1,0:T(8,128)S(1)}, u32[]{:S(2)}, u32[]{:S(2)}) collective-permute-start(f32[584,128]{1,0:T(8,128)S(1)} %get-tuple-element.65), channel_id=1, source_target_pairs={{0,1},{1,2},{2,3},{3,4},{4,5},{5,6},{6,7},{7,8},{8,9},{9,10},{10,1... | collective-permute-start | bytes 897032 | tf_op jit(solution)/shard_map/ppermute | solution.py:291
  30.2 30.8 %collective-permute-start.4 = (f32[584,128]{1,0:T(8,128)S(1)}, f32[584,128]{1,0:T(8,128)S(1)}, u32[]{:S(2)}, u32[]{:S(2)}) collective-permute-start(f32[584,128]{1,0:T(8,128)S(1)} %get-tuple-element.64), channel_id=1, source_target_pairs={{0,1},{1,2},{2,3},{3,4},{4,5},{5,6},{6,7},{7,8},{8,9},{9,10},{10,1... | collective-permute-start | bytes 897032 | tf_op jit(solution)/shard_map/ppermute | solution.py:291
  35.1 0.7 copy-start.1
  37.4 31.3 %collective-permute-start.6 = (f32[456,128]{1,0:T(8,128)S(1)}, f32[456,128]{1,0:T(8,128)S(1)}, u32[]{:S(2)}, u32[]{:S(2)}) collective-permute-start(f32[456,128]{1,0:T(8,128)S(1)} %get-tuple-element.68), channel_id=1, source_target_pairs={{0,386},{1,387},{2,384},{3,385},{4,390},{5,391},{6,388},{7,389},{8... | collective-permute-start | bytes 700424 | tf_op jit(solution)/shard_map/ppermute | solution.py:288
  40.5 39.6 %collective-permute-start.3 = (f32[456,128]{1,0:T(8,128)S(1)}, f32[456,128]{1,0:T(8,128)S(1)}, u32[]{:S(2)}, u32[]{:S(2)}) collective-permute-start(f32[456,128]{1,0:T(8,128)S(1)} %collective-permute-done.2.refs_1_), channel_id=1, source_target_pairs={{386,1},{387,2},{384,3},{385,4},{390,5},{391,6},{388,7},{389,8},{3... | collective-permute-start | bytes 700424 | tf_op jit(solution)/shard_map/ppermute | solution.py:289
  50.9 37.7 %collective-permute-start.9 = (f32[584,128]{1,0:T(8,128)S(1)}, f32[584,128]{1,0:T(8,128)S(1)}, u32[]{:S(2)}, u32[]{:S(2)}) collective-permute-start(f32[584,128]{1,0:T(8,128)S(1)} %get-tuple-element.74), channel_id=1, source_target_pairs={{0,1},{1,2},{2,3},{3,4},{4,5},{5,6},{6,7},{7,8},{8,9},{9,10},{10,1... | collective-permute-start | bytes 897032 | tf_op jit(solution)/shard_map/ppermute | solution.py:291
  61.8 29.6 %collective-permute-start.8 = (f32[584,128]{1,0:T(8,128)S(1)}, f32[584,128]{1,0:T(8,128)S(1)}, u32[]{:S(2)}, u32[]{:S(2)}) collective-permute-start(f32[584,128]{1,0:T(8,128)S(1)} %get-tuple-element.73), channel_id=1, source_target_pairs={{0,1},{1,2},{2,3},{3,4},{4,5},{5,6},{6,7},{7,8},{8,9},{9,10},{10,1... | collective-permute-start | bytes 897032 | tf_op jit(solution)/shard_map/ppermute | solution.py:291
  68.8 26.9 %collective-permute-start.7 = (f32[456,128]{1,0:T(8,128)S(1)}, f32[456,128]{1,0:T(8,128)S(1)}, u32[]{:S(2)}, u32[]{:S(2)}) collective-permute-start(f32[456,128]{1,0:T(8,128)S(1)} %collective-permute-done.6.refs_1_), channel_id=1, source_target_pairs={{386,1},{387,2},{384,3},{385,4},{390,5},{391,6},{388,7},{389,8},{3... | collective-permute-start | bytes 700424 | tf_op jit(solution)/shard_map/ppermute | solution.py:289
  80.9 15.5 %collective-permute-start.10 = (f32[456,128]{1,0:T(8,128)S(1)}, f32[456,128]{1,0:T(8,128)S(1)}, u32[]{:S(2)}, u32[]{:S(2)}) collective-permute-start(f32[456,128]{1,0:T(8,128)S(1)} %get-tuple-element.78), channel_id=1, source_target_pairs={{0,1},{1,2},{2,3},{3,4},{4,5},{5,6},{6,7},{7,8},{8,9},{9,10},{10,1... | collective-permute-start | bytes 700424 | tf_op jit(solution)/shard_map/ppermute | solution.py:291
  89.5 15.0 %collective-permute-start.13 = (f32[584,128]{1,0:T(8,128)S(1)}, f32[584,128]{1,0:T(8,128)S(1)}, u32[]{:S(2)}, u32[]{:S(2)}) collective-permute-start(f32[584,128]{1,0:T(8,128)S(1)} %get-tuple-element.84), channel_id=1, source_target_pairs={{0,48},{1,49},{2,50},{3,51},{4,52},{5,53},{6,54},{7,55},{8,56},{9,... | collective-permute-start | bytes 897032 | tf_op jit(solution)/shard_map/ppermute | solution.py:286
  92.2 12.3 %collective-permute-start.14 = (f32[584,128]{1,0:T(8,128)S(1)}, f32[584,128]{1,0:T(8,128)S(1)}, u32[]{:S(2)}, u32[]{:S(2)}) collective-permute-start(f32[584,128]{1,0:T(8,128)S(1)} %get-tuple-element.85), channel_id=1, source_target_pairs={{0,48},{1,49},{2,50},{3,51},{4,52},{5,53},{6,54},{7,55},{8,56},{9,... | collective-permute-start | bytes 897032 | tf_op jit(solution)/shard_map/ppermute | solution.py:286
  97.2 9.5 %collective-permute-start.12 = (f32[456,128]{1,0:T(8,128)S(1)}, f32[456,128]{1,0:T(8,128)S(1)}, u32[]{:S(2)}, u32[]{:S(2)}) collective-permute-start(f32[456,128]{1,0:T(8,128)S(1)} %get-tuple-element.83), channel_id=1, source_target_pairs={{0,48},{1,49},{2,50},{3,51},{4,52},{5,53},{6,54},{7,55},{8,56},{9,... | collective-permute-start | bytes 700424 | tf_op jit(solution)/shard_map/ppermute | solution.py:286
  99.2 10.1 %collective-permute-start.11 = (f32[456,128]{1,0:T(8,128)S(1)}, f32[456,128]{1,0:T(8,128)S(1)}, u32[]{:S(2)}, u32[]{:S(2)}) collective-permute-start(f32[456,128]{1,0:T(8,128)S(1)} %get-tuple-element.82), channel_id=1, source_target_pairs={{0,48},{1,49},{2,50},{3,51},{4,52},{5,53},{6,54},{7,55},{8,56},{9,... | collective-permute-start | bytes 700424 | tf_op jit(solution)/shard_map/ppermute | solution.py:286
